TPU v7x, 32 devices: a whole 2x2x4 slice. The times are simulated.
32 devices in a mesh: dp: 2 (over y), fsdp: 4 (over z), tensor: 4 (over x, core).
Axes of the slice: x: 2, y: 2, z: 4, core: 2. Of those that a mesh axis runs over, the one named last changes fastest.
Arguments:
- weight: float32 [4096, 4096], P('fsdp', 'tensor'), may hold values from -0.000234375 to 0.000234375
- momentum: bfloat16 [2, 4096, 4096], P('dp', 'fsdp', 'tensor'), may hold values from -8 to 8
- grads: bfloat16 [2, 2, 4096, 4096], P('dp', None, 'fsdp', 'tensor'), may hold values from -8 to 8
- right_factor: float32 [64, 4096], P(None, 'tensor'), may hold values from -1 to 1
Outputs:
- new_weight: float32 [4096, 4096], P('fsdp', 'tensor')
- new_momentum: bfloat16 [2, 4096, 4096], P('dp', 'fsdp', 'tensor')
- new_right: float32 [64, 4096], P(None, 'tensor')
All inputs are finite; a program needn't handle non-finite values.
Results may differ from a plain program's by a relative error of at most 0.001.
Values sent between devices are 32-bit elements; how exact they have to be, the bound alone decides.
No kernel may reach another device: no remote copies, remote signals or barrier semaphores. Data moves between devices by JAX's collectives and lax.ppermute only.
A program may use at most 64 MiB of HBM per device.

v0:
```python
import functools
import math

import jax
import jax.numpy as jnp
from jax import lax
from jax.experimental import pallas as pl
from jax.experimental.pallas import tpu as pltpu
from jax.sharding import PartitionSpec as P


ROWS = 4096
COLS = 4096

decay_part = 0.05
learn_rate = 0.02
epsilon = 1e-06

F32 = jnp.float32
BF16 = jnp.bfloat16
NT = (((1,), (1,)), ((), ()))
NN = (((1,), (0,)), ((), ()))
TN = (((0,), (0,)), ((), ()))


def dot(a, b, dims=NN):
    return lax.dot_general(a, b, dims, preferred_element_type=F32)


def exact_dot(a, b, dims=NN):
    return lax.dot_general(
        a, b, dims, precision=lax.Precision.HIGHEST, preferred_element_type=F32
    )


def parts_of(x, count):
    parts = []
    for _ in range(count):
        part = x.astype(BF16)
        parts.append(part)
        x = x - part.astype(F32)
    return parts


def inverse_lower(gram, floor=None):
    rank = gram.shape[0]
    rows = lax.broadcasted_iota(jnp.int32, (rank, rank), 0)
    cols = lax.broadcasted_iota(jnp.int32, (rank, rank), 1)
    unit = jnp.where(rows == cols, 1.0, 0.0).astype(F32)
    both = jnp.concatenate([unit, gram], axis=1)
    height = 8
    full = (height, 2 * rank)
    blocks = [both[i : i + height] for i in range(0, rank, height)]
    sub = lax.broadcasted_iota(jnp.int32, full, 0)

    def spread(x, s):
        return jnp.broadcast_to(x[s : s + 1, :], full)

    if floor is not None:
        least = floor * jnp.sum(jnp.where(rows == cols, gram, 0.0), axis=1, keepdims=True)
        least = jnp.broadcast_to(least, (rank, 2 * rank))

    pivots = []
    for at in range(rank // height):
        live = blocks[at:]
        columns = []
        for j in range(height):
            k = rank + at * height + j
            columns.append(
                [jnp.where(sub >= 0, jnp.broadcast_to(x[:, k : k + 1], full), 0.0) for x in live]
            )
        found = jnp.ones(full, F32)
        for k in range(height):
            pivot = spread(columns[k][0], k)
            if floor is not None:
                pivot = jnp.maximum(pivot, spread(least[at * height : (at + 1) * height], k))
            found = jnp.where(sub == k, pivot, found)
            over = 1.0 / pivot
            line = spread(live[0], k) * over
            for j in range(k + 1, height):
                more = spread(columns[j][0], k) * over
                for i in range(len(live)):
                    columns[j][i] = columns[j][i] - columns[k][i] * more
            for i in range(len(live)):
                column = columns[k][i]
                if i == 0:
                    if k == height - 1:
                        continue
                    column = jnp.where(sub > k, column, 0.0)
                live[i] = live[i] - column * line
        blocks[at:] = live
        pivots.append(found)
    both = jnp.concatenate(blocks, axis=0)
    return both[:, :rank] / jnp.sqrt(jnp.concatenate(pivots, axis=0)[:, :rank])


VMEM_SPEC = pl.BlockSpec(memory_space=pltpu.VMEM)
SMEM_SPEC = pl.BlockSpec(memory_space=pltpu.SMEM)
HBM_SPEC = pl.BlockSpec(memory_space=pltpu.HBM)


GRANT = pltpu.CompilerParams(vmem_limit_bytes=20 * 1024 * 1024)


def left_out(x):
    return pltpu.with_memory_space_constraint(x, pltpu.HBM)


def held(x):
    return pltpu.with_memory_space_constraint(x, pltpu.VMEM)


def raw_terms(parts, m_ref, g_ref, at):
    rank = parts.shape[0] // 3
    total = dot(parts, m_ref[0, at, :], NT)
    for i in range(g_ref.shape[1]):
        total += dot(parts, g_ref[0, i, at, :], NT)
    return total[:rank] + total[rank : 2 * rank] + total[2 * rank :]


def rows_of(half, piece, pieces, height):
    return pl.ds(pl.multiple_of((half * pieces + piece) * height, height), height)


def load_kernel(
    replicas, ids_ref, m_hbm, g_hbm, r_hbm, m_ref, g_ref, r_ref, parts_ref, out_ref, sems, r_sem
):
    pieces, _, height = out_ref.shape
    loops = g_hbm.shape[1]
    first = pltpu.make_async_copy(r_hbm, r_ref, r_sem)
    first.start()
    copies = []
    for piece in range(2 * pieces):
        half = ids_ref[0] if piece >= pieces else 1 - ids_ref[0]
        at = rows_of(half, piece % pieces, pieces, height)
        group = [
            pltpu.make_async_copy(m_hbm.at[0, at, :], m_ref.at[0, at, :], sems.at[piece, loops])
        ]
        for i in range(loops):
            group.append(
                pltpu.make_async_copy(
                    g_hbm.at[0, i, at, :], g_ref.at[0, i, at, :], sems.at[piece, i]
                )
            )
        for copy in group:
            copy.start()
        copies.append(group)
    first.wait()
    parts = jnp.concatenate(parts_of(r_ref[...], 3), axis=0)
    parts_ref[...] = parts
    for piece in range(pieces):
        for copy in copies[piece]:
            copy.wait()
        at = rows_of(1 - ids_ref[0], piece, pieces, height)
        out_ref[piece] = raw_terms(parts, m_ref, g_ref, at) / replicas
    for group in copies[pieces:]:
        for copy in group:
            copy.wait()


def load(ids, momentum, grads, right_factor, pieces, replicas):
    rank, cols = right_factor.shape
    loops, rows = grads.shape[1:3]
    return pl.pallas_call(
        functools.partial(load_kernel, replicas),
        out_shape=[
            pltpu.VMEM(momentum.shape, momentum.dtype),
            pltpu.VMEM(grads.shape, grads.dtype),
            pltpu.VMEM((rank, cols), F32),
            pltpu.VMEM((3 * rank, cols), BF16),
            jax.ShapeDtypeStruct((pieces, rank, rows // (2 * pieces)), F32),
        ],
        in_specs=[SMEM_SPEC] + [HBM_SPEC] * 3,
        out_specs=[VMEM_SPEC] * 5,
        scratch_shapes=[
            pltpu.SemaphoreType.DMA((2 * pieces, loops + 1)),
            pltpu.SemaphoreType.DMA,
        ],
        compiler_params=GRANT,
        name="load",
    )(ids, left_out(momentum), left_out(grads), left_out(right_factor))


def basis_kernel(r_ref, out_ref):
    out_ref[...] = inverse_lower(exact_dot(r_ref[...], r_ref[...], NT), 1e-5)


def basis(right_factor):
    rank = right_factor.shape[0]
    return pl.pallas_call(
        basis_kernel,
        out_shape=jax.ShapeDtypeStruct((rank, rank), F32),
        in_specs=[VMEM_SPEC],
        out_specs=VMEM_SPEC,
        compiler_params=GRANT,
        name="basis",
    )(held(right_factor))


def raw_kernel(replicas, ids_ref, m_ref, g_ref, parts_ref, out_ref):
    pieces, _, height = out_ref.shape
    parts = parts_ref[...]
    for piece in range(pieces):
        at = rows_of(ids_ref[0], piece, pieces, height)
        out_ref[piece] = raw_terms(parts, m_ref, g_ref, at) / replicas


def raw_half(ids, momentum, grads, parts, pieces, replicas):
    rank = parts.shape[0] // 3
    height = grads.shape[2] // (2 * pieces)
    return pl.pallas_call(
        functools.partial(raw_kernel, replicas),
        out_shape=jax.ShapeDtypeStruct((pieces, rank, height), F32),
        in_specs=[SMEM_SPEC] + [VMEM_SPEC] * 3,
        out_specs=VMEM_SPEC,
        compiler_params=GRANT,
        name="raw_half",
    )(ids, held(momentum), held(grads), held(parts))


def products_kernel(
    size, ids_ref, basis_ref, own_ref, other_ref, m_ref, g_ref, left_ref, *rest
):
    sends, (pieces_ref,) = rest[:size], rest[size:]
    half, rank, height = own_ref.shape
    cols = m_ref.shape[2]
    total = gram = None
    for q in range(2 * half):
        piece = jnp.where(ids_ref[0] == q // half, own_ref[q % half], other_ref[q % half])
        piece = exact_dot(basis_ref[...], piece)
        left_ref[q] = piece
        parts = jnp.concatenate(parts_of(piece, 3), axis=0)
        at = slice(q * height, (q + 1) * height)
        more = dot(parts, m_ref[0, at, :])
        for i in range(g_ref.shape[1]):
            more += dot(parts, g_ref[0, i, at, :])
        total = more if total is None else total + more
        more = exact_dot(piece, piece, NT)
        gram = more if gram is None else gram + more
    total = total[:rank] + total[rank : 2 * rank] + total[2 * rank :]
    width = cols // size
    for j in range(size):
        pieces_ref[j] = total[:, j * width : (j + 1) * width]
    for s, send in enumerate(sends):
        send[:rank, :] = pieces_ref[jnp.bitwise_xor(ids_ref[1], s)]
        pack(send, gram)


def pack(ref, gram):
    rank = gram.shape[0]
    side = ref.shape[1] // rank
    height = rank // side
    for j in range(side):
        ref[rank:, j * rank : (j + 1) * rank] = gram[j * height : (j + 1) * height]


def packed_rows(rank, width):
    side = width // rank
    assert side * rank == width and rank % side == 0
    return rank + rank // side


def products(ids, base, own, other, momentum, grads, size):
    half, rank, height = own.shape
    width = grads.shape[3] // size
    return pl.pallas_call(
        functools.partial(products_kernel, size),
        out_shape=[jax.ShapeDtypeStruct((2 * half, rank, height), F32)]
        + [jax.ShapeDtypeStruct((packed_rows(rank, width), width), F32)] * size,
        in_specs=[SMEM_SPEC] + [VMEM_SPEC] * 5,
        out_specs=[VMEM_SPEC] * (1 + size),
        scratch_shapes=[pltpu.VMEM((size, rank, width), F32)],
        compiler_params=GRANT,
        name="products",
    )(ids, base, own, other, held(momentum), held(grads))


def first_kernel(size, *refs):
    grams, left_ref, step_ref, first_ref, gram_ref = refs[:size], *refs[size:]
    rank = left_ref.shape[1]
    gram = grams[0][rank:, :]
    for ref in grams[1:]:
        gram = gram + ref[rank:, :]
    side = gram.shape[1] // rank
    gram = jnp.concatenate([gram[:, j * rank : (j + 1) * rank] for j in range(side)], axis=0)
    step = inverse_lower(gram)
    step_ref[...] = step
    total = None
    for q in range(left_ref.shape[0]):
        first = exact_dot(step, left_ref[q])
        first_ref[q] = first
        more = exact_dot(first, first, NT)
        total = more if total is None else total + more
    gram_ref[...] = total


def first_sweep(grams, left):
    rank = left.shape[1]
    square = jax.ShapeDtypeStruct((rank, rank), F32)
    return pl.pallas_call(
        functools.partial(first_kernel, len(grams)),
        out_shape=[square, jax.ShapeDtypeStruct(left.shape, F32), square],
        compiler_params=GRANT,
        name="first_sweep",
    )(*grams, left)


def second_kernel(size, *refs):
    grams, (step_ref, first_ref, left_ref, both_ref) = refs[:size], refs[size:]
    gram = grams[0][...]
    for ref in grams[1:]:
        gram = gram + ref[...]
    step = inverse_lower(gram)
    for q in range(first_ref.shape[0]):
        left_ref[q] = exact_dot(step, first_ref[q])
    both_ref[...] = exact_dot(step, step_ref[...])


def second_sweep(grams, step, first):
    return pl.pallas_call(
        functools.partial(second_kernel, len(grams)),
        out_shape=[
            jax.ShapeDtypeStruct(first.shape, F32),
            jax.ShapeDtypeStruct(step.shape, F32),
        ],
        compiler_params=GRANT,
        name="second_sweep",
    )(*grams, step, first)


def shared_kernel(size, replicas, ids_ref, both_ref, *refs):
    own, other, (shared_ref, sums_ref) = refs[:size], refs[size : 2 * size], refs[2 * size :]
    both = both_ref[...]
    sums = None
    for s in range(size):
        shared = exact_dot(both, own[s][...] + other[s][...]) / replicas
        shared_ref[jnp.bitwise_xor(ids_ref[1], s)] = shared
        squares = shared * shared
        lanes = min(128, squares.shape[1])
        for at in range(0, squares.shape[1], lanes):
            more = squares[:, at : at + lanes]
            sums = more if sums is None else sums + more
    sums_ref[...] = sums


def shared_step(ids, both, own, other, replicas):
    size = len(own)
    rank, width = own[0].shape
    return pl.pallas_call(
        functools.partial(shared_kernel, size, replicas),
        out_shape=[
            jax.ShapeDtypeStruct((size, rank, width), F32),
            jax.ShapeDtypeStruct((rank, min(128, width)), F32),
        ],
        in_specs=[SMEM_SPEC] + [VMEM_SPEC] * (1 + 2 * size),
        out_specs=[VMEM_SPEC] * 2,
        compiler_params=GRANT,
        name="shared_step",
    )(ids, both, *own, *other)


def tall(x):
    hi, lo = parts_of(x, 2)
    return jnp.concatenate([hi, lo, hi, lo], axis=0)


def wide(x):
    hi, lo = parts_of(x, 2)
    return jnp.concatenate([hi, hi, lo, lo], axis=0)


def momentum_kernel(size, ids_ref, left_ref, both_ref, *refs):
    own, refs = refs[:size], refs[size:]
    m_ref, g_ref, out_ref, right_ref, slots_ref, sems = refs
    for s in range(size):
        right_ref[jnp.bitwise_xor(ids_ref[1], s)] = wide(exact_dot(both_ref[...], own[s][...]))
    width = right_ref.shape[2]
    pieces, _, height = left_ref.shape
    copies = []
    for q in range(pieces):
        left = tall(left_ref[q])
        down = slice(q * height, (q + 1) * height)
        for j in range(size):
            at = slice(j * width, (j + 1) * width)
            blended = g_ref[0, 0, down, at].astype(F32)
            for i in range(1, g_ref.shape[1]):
                blended = blended + g_ref[0, i, down, at].astype(F32)
            blended = m_ref[0, down, at].astype(F32) + blended
            projected = dot(left, right_ref[j], TN)
            slots_ref[q, :, at] = (blended - decay_part * projected).astype(BF16)
        copies.append(
            pltpu.make_async_copy(slots_ref.at[q], out_ref.at[0, down, :], sems.at[q])
        )
        copies[-1].start()
    for copy in copies:
        copy.wait()


def momentum_step(ids, left, both, own, momentum, grads):
    size = len(own)
    pieces, rank, height = left.shape
    width = own[0].shape[1]
    cols = grads.shape[3]
    return pl.pallas_call(
        functools.partial(momentum_kernel, size),
        out_shape=jax.ShapeDtypeStruct(momentum.shape, BF16),
        in_specs=[SMEM_SPEC] + [VMEM_SPEC] * (4 + size),
        out_specs=HBM_SPEC,
        scratch_shapes=[
            pltpu.VMEM((size, 4 * rank, width), BF16),
            pltpu.VMEM((pieces, height, cols), BF16),
            pltpu.SemaphoreType.DMA((pieces,)),
        ],
        compiler_params=GRANT,
        name="momentum_step",
    )(ids, left, both, *own, held(momentum), held(grads))


def weight_kernel(count, scale, left_ref, shared_ref, *refs):
    sums, refs = refs[:count], refs[count:]
    w_ref, out_ref, new_right_ref, right_ref, slots_ref, sems = refs
    size, _, width = right_ref.shape
    total = sums[0][...]
    for ref in sums[1:]:
        total = total + ref[...]
    norm = jnp.sqrt(jnp.sum(total, axis=1, keepdims=True) + epsilon)
    for j in range(size):
        new_right = shared_ref[j] / norm
        new_right_ref[:, j * width : (j + 1) * width] = new_right
        right_ref[j] = wide(new_right)
    pieces, _, height = left_ref.shape
    copies = []
    for q in range(pieces):
        left = tall(left_ref[q])
        down = slice(q * height, (q + 1) * height)
        for j in range(size):
            at = slice(j * width, (j + 1) * width)
            slots_ref[q, :, at] = w_ref[down, at] - scale * dot(left, right_ref[j], TN)
        copies.append(pltpu.make_async_copy(slots_ref.at[q], out_ref.at[down, :], sems.at[q]))
        copies[-1].start()
    for copy in copies:
        copy.wait()


def weight_step(left, shared, sums, weight, scale):
    pieces, rank, height = left.shape
    size, _, width = shared.shape
    _, cols = weight.shape
    return pl.pallas_call(
        functools.partial(weight_kernel, len(sums), scale),
        out_shape=[
            jax.ShapeDtypeStruct(weight.shape, F32),
            jax.ShapeDtypeStruct((rank, cols), F32),
        ],
        in_specs=[VMEM_SPEC] * (3 + len(sums)),
        out_specs=[HBM_SPEC, VMEM_SPEC],
        scratch_shapes=[
            pltpu.VMEM((size, 4 * rank, width), BF16),
            pltpu.VMEM((pieces, height, cols), F32),
            pltpu.SemaphoreType.DMA((pieces,)),
        ],
        compiler_params=GRANT,
        name="weight_step",
    )(left, shared, *sums, held(weight))


def swap(x, axis, bit):
    size = lax.axis_size(axis)
    return lax.ppermute(x, axis, [(i, i ^ bit) for i in range(size)])


def bits_of(axis):
    size = lax.axis_size(axis)
    assert size & (size - 1) == 0
    return [(axis, 1 << i) for i in range(size.bit_length() - 1)]


def step(weight, momentum, grads, right_factor):
    replicas = lax.axis_size("dp")
    size = lax.axis_size("fsdp")
    others = range(1, size)
    rank = right_factor.shape[0]
    near = lax.axis_index("tensor") % 2
    ids = jnp.stack([near, lax.axis_index("fsdp")]).astype(jnp.int32)

    momentum, grads, right_factor, parts, sent = load(
        ids, momentum, grads, right_factor, 2, replicas
    )
    sent = swap(sent, "tensor", 1)
    kept = raw_half(ids, momentum, grads, parts, 2, replicas)
    own = kept + sent
    right_factor, own = lax.optimization_barrier((right_factor, own))
    base = basis(right_factor)
    for axis, bit in bits_of("tensor")[1:] + bits_of("dp"):
        own = own + swap(own, axis, bit)
    other = swap(own, "tensor", 1)

    left_raw, *sends = products(ids, base, own, other, momentum, grads, size)
    got = [sends[0]] + [swap(sends[s], "fsdp", s) for s in others]
    mine = sum(g[:rank] for g in got)
    pieces = [mine] + [swap(mine, "fsdp", s) for s in others]

    weight, left_raw = lax.optimization_barrier((weight, left_raw))
    factor, first, gram = first_sweep(got, left_raw)
    grams = [gram] + [swap(gram, "fsdp", s) for s in others]

    ours, theirs = [], []
    for piece in pieces:
        for axis, bit in bits_of("dp")[:-1]:
            piece = piece + swap(piece, axis, bit)
        ours.append(piece)
        theirs.append(swap(piece, *bits_of("dp")[-1]))

    left, both = second_sweep(grams, factor, first)
    shared, sums = shared_step(ids, both, ours, theirs, replicas)
    sums_all = [sums] + [swap(sums, "tensor", s) for s in range(1, lax.axis_size("tensor"))]
    new_momentum = momentum_step(ids, left, both, pieces, momentum, grads)
    scale = learn_rate * math.sqrt(ROWS / COLS)
    new_weight, new_right = weight_step(left, shared, sums_all, weight, scale)
    return (new_weight, new_momentum, new_right)


def solution(mesh):
    placed = (
        P("fsdp", "tensor"),
        P("dp", "fsdp", "tensor"),
        P("dp", None, "fsdp", "tensor"),
        P(None, "tensor"),
    )
    return jax.shard_map(
        step,
        mesh=mesh,
        in_specs=placed,
        out_specs=(P("fsdp", "tensor"), P("dp", "fsdp", "tensor"), P(None, "tensor")),
        check_vma=False,
    )
```

profile of v0, /device:TPU:0, one launch (start us, length us, event | category | flops | bytes accessed | tf_op | source)
XLA Modules:
  0.0 75.9 jit_solution(9773712085679527452)
XLA Ops:
  0.7 4.1 %load.1 = (bf16[1,1024,1024]{2,1,0:T(8,128)(2,1)S(1)}, bf16[1,2,1024,1024]{3,2,1,0:T(8,128)(2,1)S(1)}, f32[64,1024]{1,0:T(8,128)S(1)}, bf16[192,1024]{1,0:T(8,128)(2,1)S(1)}, f32[2,64,256]{2,1,0:T(8,128)S(1)}) custom-call(s32[2]{0:T(128)S(1)} %pad_add_fusion.ids_ref, bf16[1,1024,1024]{2,1,0:T(8,128)(2,1)} %m_hbm.1, bf16[1,2,1024,1024]{3,2,1,0:T(8,128)(2,1)} %g_hbm.1, ...), custom_call_target="tpu_custom_call" | custom-call | tf_op jit(solution)/shard_map/load/pallas_call | solution.py:164
  4.8 0.6 collective-permute-start
  5.4 1.7 %raw_half.1 = f32[2,64,256]{2,1,0:T(8,128)S(1)} custom-call(s32[2]{0:T(128)S(1)} %pad_add_fusion.ids_ref, bf16[1,1024,1024]{2,1,0:T(8,128)(2,1)S(1)} %get-tuple-element.27.m_ref.refs_4_, bf16[1,2,1024,1024]{3,2,1,0:T(8,128)(2,1)S(1)} %get-tuple-element.28.g_ref.refs_5_, bf16[192,1024]{1,0:T(8,128)(2,1)S(1)} %get-tuple-element.29.parts_ref), custom_call_target="tpu_custom_call" | custom-call | tf_op jit(solution)/shard_map/raw_half/pallas_call | solution.py:211
  7.2 2.6 %collective-permute-start.1 = (f32[2,64,256]{2,1,0:T(8,128)S(1)}, f32[2,64,256]{2,1,0:T(8,128)S(1)}, u32[]{:S(2)}, u32[]{:S(2)}) collective-permute-start(f32[2,64,256]{2,1,0:T(8,128)S(1)} %add.23), channel_id=1, source_target_pairs={{0,2},{1,3},{2,0},{3,1},{4,6},{5,7},{6,4},{7,5},{8,10},{9,11},{10,... | collective-permute-start | bytes 393224 | tf_op jit(solution)/shard_map/ppermute | solution.py:469
  9.7 4.2 %collective-permute-done.1 = f32[2,64,256]{2,1,0:T(8,128)S(1)} collective-permute-done((f32[2,64,256]{2,1,0:T(8,128)S(1)}, f32[2,64,256]{2,1,0:T(8,128)S(1)}, u32[]{:S(2)}, u32[]{:S(2)}) %collective-permute-start.1) | collective-permute-done | bytes 131104 | tf_op jit(solution)/shard_map/ppermute | solution.py:469
  13.9 1.8 %collective-permute-start.2 = (f32[2,64,256]{2,1,0:T(8,128)S(1)}, f32[2,64,256]{2,1,0:T(8,128)S(1)}, u32[]{:S(2)}, u32[]{:S(2)}) collective-permute-start(f32[2,64,256]{2,1,0:T(8,128)S(1)} %add.24), channel_id=1, source_target_pairs={{0,16},{16,0},{1,17},{17,1},{2,18},{18,2},{3,19},{19,3},{4,20},{20... | collective-permute-start | bytes 393224 | tf_op jit(solution)/shard_map/ppermute | solution.py:469
  15.7 3.5 %collective-permute-done.2 = f32[2,64,256]{2,1,0:T(8,128)S(1)} collective-permute-done((f32[2,64,256]{2,1,0:T(8,128)S(1)}, f32[2,64,256]{2,1,0:T(8,128)S(1)}, u32[]{:S(2)}, u32[]{:S(2)}) %collective-permute-start.2) | collective-permute-done | bytes 131104 | tf_op jit(solution)/shard_map/ppermute | solution.py:469
  19.4 2.0 %basis.1.basis_ref = f32[64,64]{1,0:T(8,128)S(1)} custom-call(f32[64,1024]{1,0:T(8,128)S(1)} %get-tuple-element.31.r_ref), custom_call_target="tpu_custom_call" | custom-call | tf_op jit(solution)/shard_map/basis/pallas_call | solution.py:190
  21.5 3.0 %products.1 = (f32[4,64,256]{2,1,0:T(8,128)S(1)}, f32[80,256]{1,0:T(8,128)S(1)}, f32[80,256]{1,0:T(8,128)S(1)}, f32[80,256]{1,0:T(8,128)S(1)}, f32[80,256]{1,0:T(8,128)S(1)}) custom-call(s32[2]{0:T(128)S(1)} %pad_add_fusion.ids_ref, f32[64,64]{1,0:T(8,128)S(1)} %basis.1.basis_ref, f32[2,64,256]{2,1,0:T(8,128)S(1)} %add.25.own_ref, ...), custom_call_target="tpu_custom_call" | custom-call | tf_op jit(solution)/shard_map/products/pallas_call | solution.py:266
  24.4 1.6 %collective-permute-start.4 = (f32[80,256]{1,0:T(8,128)S(1)}, f32[80,256]{1,0:T(8,128)S(1)}, u32[]{:S(2)}, u32[]{:S(2)}) collective-permute-start(f32[80,256]{1,0:T(8,128)S(1)} %get-tuple-element.34), channel_id=1, source_target_pairs={{0,4},{4,0},{8,12},{12,8},{1,5},{5,1},{9,13},{13,9},{2,6},{6,2},{1... | collective-permute-start | bytes 245768 | tf_op jit(solution)/shard_map/ppermute | solution.py:469
  26.0 2.6 %collective-permute-start.5 = (f32[80,256]{1,0:T(8,128)S(1)}, f32[80,256]{1,0:T(8,128)S(1)}, u32[]{:S(2)}, u32[]{:S(2)}) collective-permute-start(f32[80,256]{1,0:T(8,128)S(1)} %get-tuple-element.35), channel_id=1, source_target_pairs={{0,8},{4,12},{8,0},{12,4},{1,9},{5,13},{9,1},{13,5},{2,10},{6,14},... | collective-permute-start | bytes 245768 | tf_op jit(solution)/shard_map/ppermute | solution.py:469
  29.3 6.2 %collective-permute-done.5.refs_2_ = f32[80,256]{1,0:T(8,128)S(1)} collective-permute-done((f32[80,256]{1,0:T(8,128)S(1)}, f32[80,256]{1,0:T(8,128)S(1)}, u32[]{:S(2)}, u32[]{:S(2)}) %collective-permute-start.5) | collective-permute-done | bytes 81952 | tf_op jit(solution)/shard_map/ppermute | solution.py:469
  35.6 1.8 %collective-permute-start.10 = (f32[64,256]{1,0:T(8,128)S(1)}, f32[64,256]{1,0:T(8,128)S(1)}, u32[]{:S(2)}, u32[]{:S(2)}) collective-permute-start(f32[64,256]{1,0:T(8,128)S(1)} %slice_add_fusion.refs_0_), channel_id=1, source_target_pairs={{0,4},{4,0},{8,12},{12,8},{1,5},{5,1},{9,13},{13,9},{2,6},{6,2},{1... | collective-permute-start | bytes 196616 | tf_op jit(solution)/shard_map/ppermute | solution.py:469
  37.4 1.5 %collective-permute-start.11 = (f32[64,256]{1,0:T(8,128)S(1)}, f32[64,256]{1,0:T(8,128)S(1)}, u32[]{:S(2)}, u32[]{:S(2)}) collective-permute-start(f32[64,256]{1,0:T(8,128)S(1)} %slice_add_fusion.refs_0_), channel_id=1, source_target_pairs={{0,8},{4,12},{8,0},{12,4},{1,9},{5,13},{9,1},{13,5},{2,10},{6,14},... | collective-permute-start | bytes 196616 | tf_op jit(solution)/shard_map/ppermute | solution.py:469
  38.9 1.1 %collective-permute-start.12 = (f32[64,256]{1,0:T(8,128)S(1)}, f32[64,256]{1,0:T(8,128)S(1)}, u32[]{:S(2)}, u32[]{:S(2)}) collective-permute-start(f32[64,256]{1,0:T(8,128)S(1)} %slice_add_fusion.refs_0_), channel_id=1, source_target_pairs={{0,12},{4,8},{8,4},{12,0},{1,13},{5,9},{9,5},{13,1},{2,14},{6,10},... | collective-permute-start | bytes 196616 | tf_op jit(solution)/shard_map/ppermute | solution.py:469
  40.0 1.5 %collective-permute-start.13 = (f32[64,256]{1,0:T(8,128)S(1)}, f32[64,256]{1,0:T(8,128)S(1)}, u32[]{:S(2)}, u32[]{:S(2)}) collective-permute-start(f32[64,256]{1,0:T(8,128)S(1)} %slice_add_fusion.refs_0_), channel_id=1, source_target_pairs={{0,16},{16,0},{1,17},{17,1},{2,18},{18,2},{3,19},{19,3},{4,20},{20... | collective-permute-start | bytes 196616 | tf_op jit(solution)/shard_map/ppermute | solution.py:469
  41.6 0.5 collective-permute-start.14
  42.1 2.3 %collective-permute-done.11.refs_2_ = f32[64,256]{1,0:T(8,128)S(1)} collective-permute-done((f32[64,256]{1,0:T(8,128)S(1)}, f32[64,256]{1,0:T(8,128)S(1)}, u32[]{:S(2)}, u32[]{:S(2)}) %collective-permute-start.11) | collective-permute-done | bytes 65568 | tf_op jit(solution)/shard_map/ppermute | solution.py:469
  44.4 1.5 %collective-permute-start.15 = (f32[64,256]{1,0:T(8,128)S(1)}, f32[64,256]{1,0:T(8,128)S(1)}, u32[]{:S(2)}, u32[]{:S(2)}) collective-permute-start(f32[64,256]{1,0:T(8,128)S(1)} %collective-permute-done.11.refs_2_), channel_id=1, source_target_pairs={{0,16},{16,0},{1,17},{17,1},{2,18},{18,2},{3,19},{19,3},{4,20},{20... | collective-permute-start | bytes 196616 | tf_op jit(solution)/shard_map/ppermute | solution.py:469
  45.9 0.7 collective-permute-start.16
  46.6 2.4 %first_sweep.1 = (f32[64,64]{1,0:T(8,128)S(1)}, f32[4,64,256]{2,1,0:T(8,128)S(1)}, f32[64,64]{1,0:T(8,128)S(1)}) custom-call(f32[80,256]{1,0:T(8,128)S(1)} %get-tuple-element.33.refs_0_, f32[80,256]{1,0:T(8,128)S(1)} %collective-permute-done.4.refs_1_, f32[80,256]{1,0:T(8,128)S(1)} %collective-permute-done.5.refs_2_, ...), custom_call_target="tpu_custom_call" | custom-call | tf_op jit(solution)/shard_map/first_sweep/pallas_call | solution.py:300
  49.1 1.3 %collective-permute-start.7 = (f32[64,64]{1,0:T(8,128)S(1)}, f32[64,64]{1,0:T(8,128)S(1)}, u32[]{:S(2)}, u32[]{:S(2)}) collective-permute-start(f32[64,64]{1,0:T(8,128)S(1)} %get-tuple-element.39.refs_0_), channel_id=1, source_target_pairs={{0,4},{4,0},{8,12},{12,8},{1,5},{5,1},{9,13},{13,9},{2,6},{6,2},{1... | collective-permute-start | bytes 49160 | tf_op jit(solution)/shard_map/ppermute | solution.py:469
  50.4 2.6 %collective-permute-done.7.refs_1_ = f32[64,64]{1,0:T(8,128)S(1)} collective-permute-done((f32[64,64]{1,0:T(8,128)S(1)}, f32[64,64]{1,0:T(8,128)S(1)}, u32[]{:S(2)}, u32[]{:S(2)}) %collective-permute-start.7) | collective-permute-done | bytes 16416 | tf_op jit(solution)/shard_map/ppermute | solution.py:469
  53.0 2.1 %collective-permute-start.8 = (f32[64,64]{1,0:T(8,128)S(1)}, f32[64,64]{1,0:T(8,128)S(1)}, u32[]{:S(2)}, u32[]{:S(2)}) collective-permute-start(f32[64,64]{1,0:T(8,128)S(1)} %get-tuple-element.39.refs_0_), channel_id=1, source_target_pairs={{0,8},{4,12},{8,0},{12,4},{1,9},{5,13},{9,1},{13,5},{2,10},{6,14},... | collective-permute-start | bytes 49160 | tf_op jit(solution)/shard_map/ppermute | solution.py:469
  55.1 2.9 %collective-permute-done.8.refs_2_ = f32[64,64]{1,0:T(8,128)S(1)} collective-permute-done((f32[64,64]{1,0:T(8,128)S(1)}, f32[64,64]{1,0:T(8,128)S(1)}, u32[]{:S(2)}, u32[]{:S(2)}) %collective-permute-start.8) | collective-permute-done | bytes 16416 | tf_op jit(solution)/shard_map/ppermute | solution.py:469
  58.1 3.3 %collective-permute-start.9 = (f32[64,64]{1,0:T(8,128)S(1)}, f32[64,64]{1,0:T(8,128)S(1)}, u32[]{:S(2)}, u32[]{:S(2)}) collective-permute-start(f32[64,64]{1,0:T(8,128)S(1)} %get-tuple-element.39.refs_0_), channel_id=1, source_target_pairs={{0,12},{4,8},{8,4},{12,0},{1,13},{5,9},{9,5},{13,1},{2,14},{6,10},... | collective-permute-start | bytes 49160 | tf_op jit(solution)/shard_map/ppermute | solution.py:469
  61.4 2.4 %collective-permute-done.9.refs_3_ = f32[64,64]{1,0:T(8,128)S(1)} collective-permute-done((f32[64,64]{1,0:T(8,128)S(1)}, f32[64,64]{1,0:T(8,128)S(1)}, u32[]{:S(2)}, u32[]{:S(2)}) %collective-permute-start.9) | collective-permute-done | bytes 16416 | tf_op jit(solution)/shard_map/ppermute | solution.py:469
  63.8 1.9 %second_sweep.1 = (f32[4,64,256]{2,1,0:T(8,128)S(1)}, f32[64,64]{1,0:T(8,128)S(1)}) custom-call(f32[64,64]{1,0:T(8,128)S(1)} %get-tuple-element.39.refs_0_, f32[64,64]{1,0:T(8,128)S(1)} %collective-permute-done.7.refs_1_, f32[64,64]{1,0:T(8,128)S(1)} %collective-permute-done.8.refs_2_, f32[64,64]{1,0:T(8,128)S(1)} %collective-permute-done.9.refs_3_, ...), custom_call_target="tpu_custom_call" | custom-call | tf_op jit(solution)/shard_map/second_sweep/pallas_call | solution.py:320
  65.8 0.9 %shared_step.1 = (f32[4,64,256]{2,1,0:T(8,128)S(1)}, f32[64,128]{1,0:T(8,128)S(1)}) custom-call(s32[2]{0:T(128)S(1)} %pad_add_fusion.ids_ref, f32[64,64]{1,0:T(8,128)S(1)} %get-tuple-element.43.both_ref, f32[64,256]{1,0:T(8,128)S(1)} %slice_add_fusion.refs_0_, f32[64,256]{1,0:T(8,128)S(1)} %collective-permute-done.10.refs_1_, ...), custom_call_target="tpu_custom_call" | custom-call | tf_op jit(solution)/shard_map/shared_step/pallas_call | solution.py:349
  66.8 2.6 %collective-permute-start.18 = (f32[64,128]{1,0:T(8,128)S(1)}, f32[64,128]{1,0:T(8,128)S(1)}, u32[]{:S(2)}, u32[]{:S(2)}) collective-permute-start(f32[64,128]{1,0:T(8,128)S(1)} %get-tuple-element.45.refs_0_), channel_id=1, source_target_pairs={{0,2},{1,3},{2,0},{3,1},{4,6},{5,7},{6,4},{7,5},{8,10},{9,11},{10,... | collective-permute-start | bytes 98312 | tf_op jit(solution)/shard_map/ppermute | solution.py:469
  69.4 3.1 %momentum_step.1 = bf16[1,1024,1024]{2,1,0:T(8,128)(2,1)} custom-call(s32[2]{0:T(128)S(1)} %pad_add_fusion.ids_ref, f32[4,64,256]{2,1,0:T(8,128)S(1)} %get-tuple-element.42.left_ref, f32[64,64]{1,0:T(8,128)S(1)} %get-tuple-element.43.both_ref, f32[64,256]{1,0:T(8,128)S(1)} %slice_add_fusion.refs_0_, f32[64,256]{1,0:T(8,128)S(1)} %collective-permute-done.10.refs_1_, ...), custom_call_target="tpu_custom_call" | custom-call | tf_op jit(solution)/shard_map/momentum_step/pallas_call | solution.py:404
  72.7 3.2 %weight_step.1 = (f32[1024,1024]{1,0:T(8,128)}, f32[64,1024]{1,0:T(8,128)}) custom-call(f32[4,64,256]{2,1,0:T(8,128)S(1)} %get-tuple-element.42.left_ref, f32[4,64,256]{2,1,0:T(8,128)S(1)} %get-tuple-element.44.shared_ref, f32[64,128]{1,0:T(8,128)S(1)} %get-tuple-element.45.refs_0_, f32[64,128]{1,0:T(8,128)S(1)} %collective-permute-done.17.refs_1_, ...), custom_call_target="tpu_custom_call" | custom-call | tf_op jit(solution)/shard_map/weight_step/pallas_call | solution.py:449
  (24 shorter events, 1.3 us)
Async XLA Ops:
  4.8 2.3 %collective-permute-start = (f32[2,64,256]{2,1,0:T(8,128)S(1)}, f32[2,64,256]{2,1,0:T(8,128)S(1)}, u32[]{:S(2)}, u32[]{:S(2)}) collective-permute-start(f32[2,64,256]{2,1,0:T(8,128)S(1)} %get-tuple-element.30), channel_id=1, source_target_pairs={{0,1},{1,0},{2,3},{3,2},{4,5},{5,4},{6,7},{7,6},{8,9},{9,8},{10,11... | collective-permute-start | bytes 393224 | tf_op jit(solution)/shard_map/ppermute | solution.py:469
  7.2 6.7 %collective-permute-start.1 = (f32[2,64,256]{2,1,0:T(8,128)S(1)}, f32[2,64,256]{2,1,0:T(8,128)S(1)}, u32[]{:S(2)}, u32[]{:S(2)}) collective-permute-start(f32[2,64,256]{2,1,0:T(8,128)S(1)} %add.23), channel_id=1, source_target_pairs={{0,2},{1,3},{2,0},{3,1},{4,6},{5,7},{6,4},{7,5},{8,10},{9,11},{10,... | collective-permute-start | bytes 393224 | tf_op jit(solution)/shard_map/ppermute | solution.py:469
  13.9 5.4 %collective-permute-start.2 = (f32[2,64,256]{2,1,0:T(8,128)S(1)}, f32[2,64,256]{2,1,0:T(8,128)S(1)}, u32[]{:S(2)}, u32[]{:S(2)}) collective-permute-start(f32[2,64,256]{2,1,0:T(8,128)S(1)} %add.24), channel_id=1, source_target_pairs={{0,16},{16,0},{1,17},{17,1},{2,18},{18,2},{3,19},{19,3},{4,20},{20... | collective-permute-start | bytes 393224 | tf_op jit(solution)/shard_map/ppermute | solution.py:469
  19.3 2.1 %collective-permute-start.3 = (f32[2,64,256]{2,1,0:T(8,128)S(1)}, f32[2,64,256]{2,1,0:T(8,128)S(1)}, u32[]{:S(2)}, u32[]{:S(2)}) collective-permute-start(f32[2,64,256]{2,1,0:T(8,128)S(1)} %add.25.own_ref), channel_id=1, source_target_pairs={{0,1},{1,0},{2,3},{3,2},{4,5},{5,4},{6,7},{7,6},{8,9},{9,8},{10,11... | collective-permute-start | bytes 393224 | tf_op jit(solution)/shard_map/ppermute | solution.py:469
  24.4 4.9 %collective-permute-start.4 = (f32[80,256]{1,0:T(8,128)S(1)}, f32[80,256]{1,0:T(8,128)S(1)}, u32[]{:S(2)}, u32[]{:S(2)}) collective-permute-start(f32[80,256]{1,0:T(8,128)S(1)} %get-tuple-element.34), channel_id=1, source_target_pairs={{0,4},{4,0},{8,12},{12,8},{1,5},{5,1},{9,13},{13,9},{2,6},{6,2},{1... | collective-permute-start | bytes 245768 | tf_op jit(solution)/shard_map/ppermute | solution.py:469
  26.0 9.5 %collective-permute-start.5 = (f32[80,256]{1,0:T(8,128)S(1)}, f32[80,256]{1,0:T(8,128)S(1)}, u32[]{:S(2)}, u32[]{:S(2)}) collective-permute-start(f32[80,256]{1,0:T(8,128)S(1)} %get-tuple-element.35), channel_id=1, source_target_pairs={{0,8},{4,12},{8,0},{12,4},{1,9},{5,13},{9,1},{13,5},{2,10},{6,14},... | collective-permute-start | bytes 245768 | tf_op jit(solution)/shard_map/ppermute | solution.py:469
  28.6 6.9 %collective-permute-start.6 = (f32[80,256]{1,0:T(8,128)S(1)}, f32[80,256]{1,0:T(8,128)S(1)}, u32[]{:S(2)}, u32[]{:S(2)}) collective-permute-start(f32[80,256]{1,0:T(8,128)S(1)} %get-tuple-element.36), channel_id=1, source_target_pairs={{0,12},{4,8},{8,4},{12,0},{1,13},{5,9},{9,5},{13,1},{2,14},{6,10},... | collective-permute-start | bytes 245768 | tf_op jit(solution)/shard_map/ppermute | solution.py:469
  35.6 6.0 %collective-permute-start.10 = (f32[64,256]{1,0:T(8,128)S(1)}, f32[64,256]{1,0:T(8,128)S(1)}, u32[]{:S(2)}, u32[]{:S(2)}) collective-permute-start(f32[64,256]{1,0:T(8,128)S(1)} %slice_add_fusion.refs_0_), channel_id=1, source_target_pairs={{0,4},{4,0},{8,12},{12,8},{1,5},{5,1},{9,13},{13,9},{2,6},{6,2},{1... | collective-permute-start | bytes 196616 | tf_op jit(solution)/shard_map/ppermute | solution.py:469
  37.4 7.0 %collective-permute-start.11 = (f32[64,256]{1,0:T(8,128)S(1)}, f32[64,256]{1,0:T(8,128)S(1)}, u32[]{:S(2)}, u32[]{:S(2)}) collective-permute-start(f32[64,256]{1,0:T(8,128)S(1)} %slice_add_fusion.refs_0_), channel_id=1, source_target_pairs={{0,8},{4,12},{8,0},{12,4},{1,9},{5,13},{9,1},{13,5},{2,10},{6,14},... | collective-permute-start | bytes 196616 | tf_op jit(solution)/shard_map/ppermute | solution.py:469
  38.9 7.0 %collective-permute-start.12 = (f32[64,256]{1,0:T(8,128)S(1)}, f32[64,256]{1,0:T(8,128)S(1)}, u32[]{:S(2)}, u32[]{:S(2)}) collective-permute-start(f32[64,256]{1,0:T(8,128)S(1)} %slice_add_fusion.refs_0_), channel_id=1, source_target_pairs={{0,12},{4,8},{8,4},{12,0},{1,13},{5,9},{9,5},{13,1},{2,14},{6,10},... | collective-permute-start | bytes 196616 | tf_op jit(solution)/shard_map/ppermute | solution.py:469
  40.0 25.7 %collective-permute-start.13 = (f32[64,256]{1,0:T(8,128)S(1)}, f32[64,256]{1,0:T(8,128)S(1)}, u32[]{:S(2)}, u32[]{:S(2)}) collective-permute-start(f32[64,256]{1,0:T(8,128)S(1)} %slice_add_fusion.refs_0_), channel_id=1, source_target_pairs={{0,16},{16,0},{1,17},{17,1},{2,18},{18,2},{3,19},{19,3},{4,20},{20... | collective-permute-start | bytes 196616 | tf_op jit(solution)/shard_map/ppermute | solution.py:469
  41.6 24.2 %collective-permute-start.14 = (f32[64,256]{1,0:T(8,128)S(1)}, f32[64,256]{1,0:T(8,128)S(1)}, u32[]{:S(2)}, u32[]{:S(2)}) collective-permute-start(f32[64,256]{1,0:T(8,128)S(1)} %collective-permute-done.10.refs_1_), channel_id=1, source_target_pairs={{0,16},{16,0},{1,17},{17,1},{2,18},{18,2},{3,19},{19,3},{4,20},{20... | collective-permute-start | bytes 196616 | tf_op jit(solution)/shard_map/ppermute | solution.py:469
  44.4 21.4 %collective-permute-start.15 = (f32[64,256]{1,0:T(8,128)S(1)}, f32[64,256]{1,0:T(8,128)S(1)}, u32[]{:S(2)}, u32[]{:S(2)}) collective-permute-start(f32[64,256]{1,0:T(8,128)S(1)} %collective-permute-done.11.refs_2_), channel_id=1, source_target_pairs={{0,16},{16,0},{1,17},{17,1},{2,18},{18,2},{3,19},{19,3},{4,20},{20... | collective-permute-start | bytes 196616 | tf_op jit(solution)/shard_map/ppermute | solution.py:469
  45.9 19.9 %collective-permute-start.16 = (f32[64,256]{1,0:T(8,128)S(1)}, f32[64,256]{1,0:T(8,128)S(1)}, u32[]{:S(2)}, u32[]{:S(2)}) collective-permute-start(f32[64,256]{1,0:T(8,128)S(1)} %collective-permute-done.12.refs_3_), channel_id=1, source_target_pairs={{0,16},{16,0},{1,17},{17,1},{2,18},{18,2},{3,19},{19,3},{4,20},{20... | collective-permute-start | bytes 196616 | tf_op jit(solution)/shard_map/ppermute | solution.py:469
  49.1 4.0 %collective-permute-start.7 = (f32[64,64]{1,0:T(8,128)S(1)}, f32[64,64]{1,0:T(8,128)S(1)}, u32[]{:S(2)}, u32[]{:S(2)}) collective-permute-start(f32[64,64]{1,0:T(8,128)S(1)} %get-tuple-element.39.refs_0_), channel_id=1, source_target_pairs={{0,4},{4,0},{8,12},{12,8},{1,5},{5,1},{9,13},{13,9},{2,6},{6,2},{1... | collective-permute-start | bytes 49160 | tf_op jit(solution)/shard_map/ppermute | solution.py:469
  53.0 5.0 %collective-permute-start.8 = (f32[64,64]{1,0:T(8,128)S(1)}, f32[64,64]{1,0:T(8,128)S(1)}, u32[]{:S(2)}, u32[]{:S(2)}) collective-permute-start(f32[64,64]{1,0:T(8,128)S(1)} %get-tuple-element.39.refs_0_), channel_id=1, source_target_pairs={{0,8},{4,12},{8,0},{12,4},{1,9},{5,13},{9,1},{13,5},{2,10},{6,14},... | collective-permute-start | bytes 49160 | tf_op jit(solution)/shard_map/ppermute | solution.py:469
  58.1 5.7 %collective-permute-start.9 = (f32[64,64]{1,0:T(8,128)S(1)}, f32[64,64]{1,0:T(8,128)S(1)}, u32[]{:S(2)}, u32[]{:S(2)}) collective-permute-start(f32[64,64]{1,0:T(8,128)S(1)} %get-tuple-element.39.refs_0_), channel_id=1, source_target_pairs={{0,12},{4,8},{8,4},{12,0},{1,13},{5,9},{9,5},{13,1},{2,14},{6,10},... | collective-permute-start | bytes 49160 | tf_op jit(solution)/shard_map/ppermute | solution.py:469
  66.7 5.8 %collective-permute-start.17 = (f32[64,128]{1,0:T(8,128)S(1)}, f32[64,128]{1,0:T(8,128)S(1)}, u32[]{:S(2)}, u32[]{:S(2)}) collective-permute-start(f32[64,128]{1,0:T(8,128)S(1)} %get-tuple-element.45.refs_0_), channel_id=1, source_target_pairs={{0,1},{1,0},{2,3},{3,2},{4,5},{5,4},{6,7},{7,6},{8,9},{9,8},{10,11... | collective-permute-start | bytes 98312 | tf_op jit(solution)/shard_map/ppermute | solution.py:469
  66.8 5.7 %collective-permute-start.18 = (f32[64,128]{1,0:T(8,128)S(1)}, f32[64,128]{1,0:T(8,128)S(1)}, u32[]{:S(2)}, u32[]{:S(2)}) collective-permute-start(f32[64,128]{1,0:T(8,128)S(1)} %get-tuple-element.45.refs_0_), channel_id=1, source_target_pairs={{0,2},{1,3},{2,0},{3,1},{4,6},{5,7},{6,4},{7,5},{8,10},{9,11},{10,... | collective-permute-start | bytes 98312 | tf_op jit(solution)/shard_map/ppermute | solution.py:469
  69.3 3.4 %collective-permute-start.19 = (f32[64,128]{1,0:T(8,128)S(1)}, f32[64,128]{1,0:T(8,128)S(1)}, u32[]{:S(2)}, u32[]{:S(2)}) collective-permute-start(f32[64,128]{1,0:T(8,128)S(1)} %get-tuple-element.45.refs_0_), channel_id=1, source_target_pairs={{0,3},{1,2},{2,1},{3,0},{4,7},{5,6},{6,5},{7,4},{8,11},{9,10},{10,... | collective-permute-start | bytes 98312 | tf_op jit(solution)/shard_map/ppermute | solution.py:469
  69.4 3.3 %copy-start = (f32[1024,1024]{1,0:T(8,128)S(1)}, f32[1024,1024]{1,0:T(8,128)}, u32[]{:S(2)}) copy-start(f32[1024,1024]{1,0:T(8,128)} %refs_4_) | copy-start | bytes 12582916
where the time goes:
time: 76 us; the launch traced here: 75.9 us
  starting transfers between devices  27.6 us (36%)
  waiting for transfers between devices  24.9 us (33%)
  Pallas kernels  22.4 us (29%)
  between operations  0.81 us (1%)
    ppermute x20, starting transfers between devices, swap(): return lax.ppermute(x, axis, [(i, i ^ bit) for i in range(size)])  27.6 us
    ppermute x20, waiting for transfers between devices, swap(): return lax.ppermute(x, axis, [(i, i ^ bit) for i in range(size)])  24.9 us
    pallas_call x1, Pallas kernels, load(): pl.pallas_call(functools.partial(load_kernel, replicas), out_shape=[pltpu...  4.11 us
    pallas_call x1, Pallas kernels, weight_step(): pl.pallas_call(functools.partial(weight_kernel, len(sums), scale), out_sh...  3.16 us
    pallas_call x1, Pallas kernels, momentum_step(): pl.pallas_call(functools.partial(momentum_kernel, size), out_shape=jax.Sh...  3.07 us
    pallas_call x1, Pallas kernels, products(): pl.pallas_call(functools.partial(products_kernel, size), out_shape=[jax.S...  2.95 us
    pallas_call x1, Pallas kernels, first_sweep(): pl.pallas_call(functools.partial(first_kernel, len(grams)), out_shape=[sq...  2.45 us
    pallas_call x1, Pallas kernels, basis(): pl.pallas_call(basis_kernel, out_shape=jax.ShapeDtypeStruct((rank, rank),...  2.05 us
  transfers between devices with their start and end apart: 20, of which 9 were waited for; matrix products, arithmetic and copies ran while one was open for 0% of the time, Pallas kernels for 15%

commit v1 on v0

--- a/solution.py
+++ b/solution.py
@@ -123,7 +123,7 @@
 
 
 def load_kernel(
-    replicas, ids_ref, m_hbm, g_hbm, r_hbm, m_ref, g_ref, r_ref, parts_ref, out_ref, sems, r_sem
+    replicas, ids_ref, m_hbm, g_hbm, r_hbm, m_ref, g_ref, r_ref, out_ref, sems, r_sem
 ):
     pieces, _, height = out_ref.shape
     loops = g_hbm.shape[1]
@@ -147,7 +147,6 @@
         copies.append(group)
     first.wait()
     parts = jnp.concatenate(parts_of(r_ref[...], 3), axis=0)
-    parts_ref[...] = parts
     for piece in range(pieces):
         for copy in copies[piece]:
             copy.wait()
@@ -167,11 +166,10 @@
             pltpu.VMEM(momentum.shape, momentum.dtype),
             pltpu.VMEM(grads.shape, grads.dtype),
             pltpu.VMEM((rank, cols), F32),
-            pltpu.VMEM((3 * rank, cols), BF16),
             jax.ShapeDtypeStruct((pieces, rank, rows // (2 * pieces)), F32),
         ],
         in_specs=[SMEM_SPEC] + [HBM_SPEC] * 3,
-        out_specs=[VMEM_SPEC] * 5,
+        out_specs=[VMEM_SPEC] * 4,
         scratch_shapes=[
             pltpu.SemaphoreType.DMA((2 * pieces, loops + 1)),
             pltpu.SemaphoreType.DMA,
@@ -197,16 +195,16 @@
     )(held(right_factor))
 
 
-def raw_kernel(replicas, ids_ref, m_ref, g_ref, parts_ref, out_ref):
+def raw_kernel(replicas, ids_ref, m_ref, g_ref, r_ref, out_ref):
     pieces, _, height = out_ref.shape
-    parts = parts_ref[...]
+    parts = jnp.concatenate(parts_of(r_ref[...], 3), axis=0)
     for piece in range(pieces):
         at = rows_of(ids_ref[0], piece, pieces, height)
         out_ref[piece] = raw_terms(parts, m_ref, g_ref, at) / replicas
 
 
-def raw_half(ids, momentum, grads, parts, pieces, replicas):
-    rank = parts.shape[0] // 3
+def raw_half(ids, momentum, grads, right_factor, pieces, replicas):
+    rank = right_factor.shape[0]
     height = grads.shape[2] // (2 * pieces)
     return pl.pallas_call(
         functools.partial(raw_kernel, replicas),
@@ -215,7 +213,7 @@
         out_specs=VMEM_SPEC,
         compiler_params=GRANT,
         name="raw_half",
-    )(ids, held(momentum), held(grads), held(parts))
+    )(ids, held(momentum), held(grads), held(right_factor))
 
 
 def products_kernel(
@@ -275,15 +273,22 @@
     )(ids, base, own, other, held(momentum), held(grads))
 
 
-def first_kernel(size, *refs):
-    grams, left_ref, step_ref, first_ref, gram_ref = refs[:size], *refs[size:]
-    rank = left_ref.shape[1]
-    gram = grams[0][rank:, :]
-    for ref in grams[1:]:
+def gram_of(refs, rank):
+    gram = refs[0][rank:, :]
+    for ref in refs[1:]:
         gram = gram + ref[rank:, :]
     side = gram.shape[1] // rank
-    gram = jnp.concatenate([gram[:, j * rank : (j + 1) * rank] for j in range(side)], axis=0)
-    step = inverse_lower(gram)
+    return jnp.concatenate([gram[:, j * rank : (j + 1) * rank] for j in range(side)], axis=0)
+
+
+def first_kernel(size, *refs):
+    got, left_ref, step_ref, first_ref, send_ref = refs[:size], *refs[size:]
+    rank = left_ref.shape[1]
+    mine = got[0][:rank, :]
+    for ref in got[1:]:
+        mine = mine + ref[:rank, :]
+    send_ref[:rank, :] = mine
+    step = inverse_lower(gram_of(got, rank))
     step_ref[...] = step
     total = None
     for q in range(left_ref.shape[0]):
@@ -291,41 +296,41 @@
         first_ref[q] = first
         more = exact_dot(first, first, NT)
         total = more if total is None else total + more
-    gram_ref[...] = total
-
-
-def first_sweep(grams, left):
+    pack(send_ref, total)
+
+
+def first_sweep(got, left):
     rank = left.shape[1]
-    square = jax.ShapeDtypeStruct((rank, rank), F32)
-    return pl.pallas_call(
-        functools.partial(first_kernel, len(grams)),
-        out_shape=[square, jax.ShapeDtypeStruct(left.shape, F32), square],
+    return pl.pallas_call(
+        functools.partial(first_kernel, len(got)),
+        out_shape=[
+            jax.ShapeDtypeStruct((rank, rank), F32),
+            jax.ShapeDtypeStruct(left.shape, F32),
+            jax.ShapeDtypeStruct(got[0].shape, F32),
+        ],
         compiler_params=GRANT,
         name="first_sweep",
-    )(*grams, left)
+    )(*got, left)
 
 
 def second_kernel(size, *refs):
-    grams, (step_ref, first_ref, left_ref, both_ref) = refs[:size], refs[size:]
-    gram = grams[0][...]
-    for ref in grams[1:]:
-        gram = gram + ref[...]
-    step = inverse_lower(gram)
+    got, (step_ref, first_ref, left_ref, both_ref) = refs[:size], refs[size:]
+    step = inverse_lower(gram_of(got, step_ref.shape[0]))
     for q in range(first_ref.shape[0]):
         left_ref[q] = exact_dot(step, first_ref[q])
     both_ref[...] = exact_dot(step, step_ref[...])
 
 
-def second_sweep(grams, step, first):
-    return pl.pallas_call(
-        functools.partial(second_kernel, len(grams)),
+def second_sweep(got, step, first):
+    return pl.pallas_call(
+        functools.partial(second_kernel, len(got)),
         out_shape=[
             jax.ShapeDtypeStruct(first.shape, F32),
             jax.ShapeDtypeStruct(step.shape, F32),
         ],
         compiler_params=GRANT,
         name="second_sweep",
-    )(*grams, step, first)
+    )(*got, step, first)
 
 
 def shared_kernel(size, replicas, ids_ref, both_ref, *refs):
@@ -333,7 +338,9 @@
     both = both_ref[...]
     sums = None
     for s in range(size):
-        shared = exact_dot(both, own[s][...] + other[s][...]) / replicas
+        rank = both.shape[0]
+        total = own[s][:rank, :] + other[s][:rank, :]
+        shared = exact_dot(both, total) / replicas
         shared_ref[jnp.bitwise_xor(ids_ref[1], s)] = shared
         squares = shared * shared
         lanes = min(128, squares.shape[1])
@@ -345,7 +352,7 @@
 
 def shared_step(ids, both, own, other, replicas):
     size = len(own)
-    rank, width = own[0].shape
+    rank, width = both.shape[0], own[0].shape[1]
     return pl.pallas_call(
         functools.partial(shared_kernel, size, replicas),
         out_shape=[
@@ -369,11 +376,32 @@
     return jnp.concatenate([hi, hi, lo, lo], axis=0)
 
 
+def blend_kernel(m_ref, g_ref, out_ref):
+    blended = g_ref[0, 0].astype(F32)
+    for i in range(1, g_ref.shape[1]):
+        blended = blended + g_ref[0, i].astype(F32)
+    out_ref[...] = m_ref[0].astype(F32) + blended
+
+
+def blend(momentum, grads):
+    return pl.pallas_call(
+        blend_kernel,
+        out_shape=pltpu.VMEM(momentum.shape[1:], F32),
+        in_specs=[VMEM_SPEC] * 2,
+        out_specs=VMEM_SPEC,
+        compiler_params=GRANT,
+        name="blend",
+    )(held(momentum), held(grads))
+
+
 def momentum_kernel(size, ids_ref, left_ref, both_ref, *refs):
     own, refs = refs[:size], refs[size:]
-    m_ref, g_ref, out_ref, right_ref, slots_ref, sems = refs
+    blended_ref, out_ref, right_ref, slots_ref, sems = refs
+    both = decay_part * both_ref[...]
     for s in range(size):
-        right_ref[jnp.bitwise_xor(ids_ref[1], s)] = wide(exact_dot(both_ref[...], own[s][...]))
+        right_ref[jnp.bitwise_xor(ids_ref[1], s)] = wide(
+            exact_dot(both, own[s][: both.shape[0], :])
+        )
     width = right_ref.shape[2]
     pieces, _, height = left_ref.shape
     copies = []
@@ -382,12 +410,8 @@
         down = slice(q * height, (q + 1) * height)
         for j in range(size):
             at = slice(j * width, (j + 1) * width)
-            blended = g_ref[0, 0, down, at].astype(F32)
-            for i in range(1, g_ref.shape[1]):
-                blended = blended + g_ref[0, i, down, at].astype(F32)
-            blended = m_ref[0, down, at].astype(F32) + blended
             projected = dot(left, right_ref[j], TN)
-            slots_ref[q, :, at] = (blended - decay_part * projected).astype(BF16)
+            slots_ref[q, :, at] = (blended_ref[down, at] - projected).astype(BF16)
         copies.append(
             pltpu.make_async_copy(slots_ref.at[q], out_ref.at[0, down, :], sems.at[q])
         )
@@ -396,15 +420,15 @@
         copy.wait()
 
 
-def momentum_step(ids, left, both, own, momentum, grads):
+def momentum_step(ids, left, both, own, blended):
     size = len(own)
     pieces, rank, height = left.shape
     width = own[0].shape[1]
-    cols = grads.shape[3]
+    rows, cols = blended.shape
     return pl.pallas_call(
         functools.partial(momentum_kernel, size),
-        out_shape=jax.ShapeDtypeStruct(momentum.shape, BF16),
-        in_specs=[SMEM_SPEC] + [VMEM_SPEC] * (4 + size),
+        out_shape=jax.ShapeDtypeStruct((1, rows, cols), BF16),
+        in_specs=[SMEM_SPEC] + [VMEM_SPEC] * (3 + size),
         out_specs=HBM_SPEC,
         scratch_shapes=[
             pltpu.VMEM((size, 4 * rank, width), BF16),
@@ -413,12 +437,12 @@
         ],
         compiler_params=GRANT,
         name="momentum_step",
-    )(ids, left, both, *own, held(momentum), held(grads))
+    )(ids, left, both, *own, held(blended))
 
 
 def weight_kernel(count, scale, left_ref, shared_ref, *refs):
     sums, refs = refs[:count], refs[count:]
-    w_ref, out_ref, new_right_ref, right_ref, slots_ref, sems = refs
+    w_ref, out_ref, new_right_out, new_right_ref, right_ref, slots_ref, sems = refs
     size, _, width = right_ref.shape
     total = sums[0][...]
     for ref in sums[1:]:
@@ -427,15 +451,16 @@
     for j in range(size):
         new_right = shared_ref[j] / norm
         new_right_ref[:, j * width : (j + 1) * width] = new_right
-        right_ref[j] = wide(new_right)
+        right_ref[j] = wide(scale * new_right)
     pieces, _, height = left_ref.shape
-    copies = []
+    copies = [pltpu.make_async_copy(new_right_ref, new_right_out, sems.at[pieces])]
+    copies[-1].start()
     for q in range(pieces):
         left = tall(left_ref[q])
         down = slice(q * height, (q + 1) * height)
         for j in range(size):
             at = slice(j * width, (j + 1) * width)
-            slots_ref[q, :, at] = w_ref[down, at] - scale * dot(left, right_ref[j], TN)
+            slots_ref[q, :, at] = w_ref[down, at] - dot(left, right_ref[j], TN)
         copies.append(pltpu.make_async_copy(slots_ref.at[q], out_ref.at[down, :], sems.at[q]))
         copies[-1].start()
     for copy in copies:
@@ -453,11 +478,12 @@
             jax.ShapeDtypeStruct((rank, cols), F32),
         ],
         in_specs=[VMEM_SPEC] * (3 + len(sums)),
-        out_specs=[HBM_SPEC, VMEM_SPEC],
+        out_specs=[HBM_SPEC, HBM_SPEC],
         scratch_shapes=[
+            pltpu.VMEM((rank, cols), F32),
             pltpu.VMEM((size, 4 * rank, width), BF16),
             pltpu.VMEM((pieces, height, cols), F32),
-            pltpu.SemaphoreType.DMA((pieces,)),
+            pltpu.SemaphoreType.DMA((pieces + 1,)),
         ],
         compiler_params=GRANT,
         name="weight_step",
@@ -473,6 +499,16 @@
     size = lax.axis_size(axis)
     assert size & (size - 1) == 0
     return [(axis, 1 << i) for i in range(size.bit_length() - 1)]
+
+
+def half_pairs():
+    count = lax.axis_size("tensor")
+    bits = [bit for _, bit in bits_of("tensor")[1:]] + [bit * count for _, bit in bits_of("dp")]
+    every = range(count * lax.axis_size("dp"))
+    return [
+        [(i, i ^ (bits[-1 - stage] if i % 2 else bits[stage])) for i in every]
+        for stage in range(len(bits))
+    ]
 
 
 def step(weight, momentum, grads, right_factor):
@@ -483,38 +519,38 @@
     near = lax.axis_index("tensor") % 2
     ids = jnp.stack([near, lax.axis_index("fsdp")]).astype(jnp.int32)
 
-    momentum, grads, right_factor, parts, sent = load(
+    momentum, grads, right_factor, sent = load(
         ids, momentum, grads, right_factor, 2, replicas
     )
     sent = swap(sent, "tensor", 1)
-    kept = raw_half(ids, momentum, grads, parts, 2, replicas)
+    kept = raw_half(ids, momentum, grads, right_factor, 2, replicas)
     own = kept + sent
     right_factor, own = lax.optimization_barrier((right_factor, own))
     base = basis(right_factor)
-    for axis, bit in bits_of("tensor")[1:] + bits_of("dp"):
-        own = own + swap(own, axis, bit)
+    for pairs in half_pairs():
+        own_in = lax.ppermute(own, ("dp", "tensor"), pairs)
+        own = own + own_in
     other = swap(own, "tensor", 1)
 
     left_raw, *sends = products(ids, base, own, other, momentum, grads, size)
+    blended = blend(momentum, grads)
     got = [sends[0]] + [swap(sends[s], "fsdp", s) for s in others]
-    mine = sum(g[:rank] for g in got)
-    pieces = [mine] + [swap(mine, "fsdp", s) for s in others]
-
     weight, left_raw = lax.optimization_barrier((weight, left_raw))
-    factor, first, gram = first_sweep(got, left_raw)
-    grams = [gram] + [swap(gram, "fsdp", s) for s in others]
+    factor, first, send = first_sweep(got, left_raw)
+    pieces = [send] + [swap(send, "fsdp", s) for s in others]
 
     ours, theirs = [], []
     for piece in pieces:
+        piece = piece[:rank]
         for axis, bit in bits_of("dp")[:-1]:
             piece = piece + swap(piece, axis, bit)
         ours.append(piece)
         theirs.append(swap(piece, *bits_of("dp")[-1]))
 
-    left, both = second_sweep(grams, factor, first)
+    left, both = second_sweep(pieces, factor, first)
     shared, sums = shared_step(ids, both, ours, theirs, replicas)
     sums_all = [sums] + [swap(sums, "tensor", s) for s in range(1, lax.axis_size("tensor"))]
-    new_momentum = momentum_step(ids, left, both, pieces, momentum, grads)
+    new_momentum = momentum_step(ids, left, both, pieces, blended)
     scale = learn_rate * math.sqrt(ROWS / COLS)
     new_weight, new_right = weight_step(left, shared, sums_all, weight, scale)
     return (new_weight, new_momentum, new_right)

time: 76 us -> 62 us (0.82)
  waiting for transfers between devices: 24.9 us -> 17.2 us
  starting transfers between devices: 27.6 us -> 21.5 us
    ppermute x20 -> x15, waiting for transfers between devices: 24.9 us -> 11.3 us  [swap(): return lax.ppermute(x, axis, [(i, i ^ bit) for i in range(size)])]
    ppermute x20 -> x15, starting transfers between devices: 27.6 us -> 16.8 us  [swap(): return lax.ppermute(x, axis, [(i, i ^ bit) for i in range(size)])]
    ppermute x0 -> x2, waiting for transfers between devices: none -> 5.89 us  [step(): own_in = lax.ppermute(own, ('dp', 'tensor'), pairs)]
    ppermute x0 -> x2, starting transfers between devices: none -> 4.67 us  [step(): own_in = lax.ppermute(own, ('dp', 'tensor'), pairs)]
    pallas_call x2 -> x3, Pallas kernels: 4.39 us -> 5.4 us  [the longest x1 2.52 us: first_sweep(): pl.pallas_call(functools.partial(first_kernel, len(got)), out_shape=[jax....]
  transfers between devices with their start and end apart: 20 -> 17, of which waited for: 9 -> 8; matrix products, arithmetic and copies ran while one was open for 0% -> 0% of each run, Pallas kernels for 15% -> 15%
where the time goes in v1:
time: 62 us; the launch traced here: 61.9 us
  Pallas kernels  22.2 us (36%)
  starting transfers between devices  21.5 us (35%)
  waiting for transfers between devices  17.2 us (28%)
  between operations  0.81 us (1%)
    ppermute x15, starting transfers between devices, swap(): return lax.ppermute(x, axis, [(i, i ^ bit) for i in range(size)])  16.8 us
    ppermute x15, waiting for transfers between devices, swap(): return lax.ppermute(x, axis, [(i, i ^ bit) for i in range(size)])  11.3 us
    ppermute x2, waiting for transfers between devices, step(): own_in = lax.ppermute(own, ('dp', 'tensor'), pairs)  5.89 us
    ppermute x2, starting transfers between devices, step(): own_in = lax.ppermute(own, ('dp', 'tensor'), pairs)  4.67 us
    pallas_call x1, Pallas kernels, load(): pl.pallas_call(functools.partial(load_kernel, replicas), out_shape=[pltpu...  4.11 us
    pallas_call x1, Pallas kernels, products(): pl.pallas_call(functools.partial(products_kernel, size), out_shape=[jax.S...  2.94 us
    pallas_call x1, Pallas kernels, momentum_step(): pl.pallas_call(functools.partial(momentum_kernel, size), out_shape=jax.Sh...  2.58 us
    pallas_call x1, Pallas kernels, first_sweep(): pl.pallas_call(functools.partial(first_kernel, len(got)), out_shape=[jax....  2.52 us
  transfers between devices with their start and end apart: 17, of which 8 were waited for; matrix products, arithmetic and copies ran while one was open for 0% of the time, Pallas kernels for 15%

profile of v1, /device:TPU:0, one launch (start us, length us, event | category | flops | bytes accessed | tf_op | source)
XLA Modules:
  0.0 61.9 jit_solution(11228261514218259673)
XLA Ops:
  0.7 4.1 %load.1 = (bf16[1,1024,1024]{2,1,0:T(8,128)(2,1)S(1)}, bf16[1,2,1024,1024]{3,2,1,0:T(8,128)(2,1)S(1)}, f32[64,1024]{1,0:T(8,128)S(1)}, f32[2,64,256]{2,1,0:T(8,128)S(1)}) custom-call(s32[2]{0:T(128)S(1)} %pad_add_fusion.ids_ref, bf16[1,1024,1024]{2,1,0:T(8,128)(2,1)} %m_hbm.1, bf16[1,2,1024,1024]{3,2,1,0:T(8,128)(2,1)} %g_hbm.1, f32[64,1024]{1,0:T(8,128)} %r_hbm.1), custom_call_target="tpu_custom_call" | custom-call | tf_op jit(solution)/shard_map/load/pallas_call | solution.py:163
  4.8 0.6 collective-permute-start
  5.4 1.7 %raw_half.1 = f32[2,64,256]{2,1,0:T(8,128)S(1)} custom-call(s32[2]{0:T(128)S(1)} %pad_add_fusion.ids_ref, bf16[1,1024,1024]{2,1,0:T(8,128)(2,1)S(1)} %get-tuple-element.26.m_ref, bf16[1,2,1024,1024]{3,2,1,0:T(8,128)(2,1)S(1)} %get-tuple-element.27.g_ref, f32[64,1024]{1,0:T(8,128)S(1)} %get-tuple-element.29.r_ref), custom_call_target="tpu_custom_call" | custom-call | tf_op jit(solution)/shard_map/raw_half/pallas_call | solution.py:209
  7.2 2.6 %collective-permute-start.1 = (f32[2,64,256]{2,1,0:T(8,128)S(1)}, f32[2,64,256]{2,1,0:T(8,128)S(1)}, u32[]{:S(2)}, u32[]{:S(2)}) collective-permute-start(f32[2,64,256]{2,1,0:T(8,128)S(1)} %add.14), channel_id=1, source_target_pairs={{0,2},{1,17},{2,0},{3,19},{16,18},{17,1},{18,16},{19,3},{4,6},{5,2... | collective-permute-start | bytes 393224 | tf_op jit(solution)/shard_map/ppermute | solution.py:531
  9.7 2.9 %collective-permute-done.1 = f32[2,64,256]{2,1,0:T(8,128)S(1)} collective-permute-done((f32[2,64,256]{2,1,0:T(8,128)S(1)}, f32[2,64,256]{2,1,0:T(8,128)S(1)}, u32[]{:S(2)}, u32[]{:S(2)}) %collective-permute-start.1) | collective-permute-done | bytes 131104 | tf_op jit(solution)/shard_map/ppermute | solution.py:531
  12.7 2.1 %collective-permute-start.2 = (f32[2,64,256]{2,1,0:T(8,128)S(1)}, f32[2,64,256]{2,1,0:T(8,128)S(1)}, u32[]{:S(2)}, u32[]{:S(2)}) collective-permute-start(f32[2,64,256]{2,1,0:T(8,128)S(1)} %add.15), channel_id=1, source_target_pairs={{0,16},{1,3},{2,18},{3,1},{16,0},{17,19},{18,2},{19,17},{4,20},{5,... | collective-permute-start | bytes 393224 | tf_op jit(solution)/shard_map/ppermute | solution.py:531
  14.8 2.9 %collective-permute-done.2 = f32[2,64,256]{2,1,0:T(8,128)S(1)} collective-permute-done((f32[2,64,256]{2,1,0:T(8,128)S(1)}, f32[2,64,256]{2,1,0:T(8,128)S(1)}, u32[]{:S(2)}, u32[]{:S(2)}) %collective-permute-start.2) | collective-permute-done | bytes 131104 | tf_op jit(solution)/shard_map/ppermute | solution.py:531
  17.8 2.0 %basis.1.basis_ref = f32[64,64]{1,0:T(8,128)S(1)} custom-call(f32[64,1024]{1,0:T(8,128)S(1)} %get-tuple-element.29.r_ref), custom_call_target="tpu_custom_call" | custom-call | tf_op jit(solution)/shard_map/basis/pallas_call | solution.py:188
  19.9 2.9 %products.1 = (f32[4,64,256]{2,1,0:T(8,128)S(1)}, f32[80,256]{1,0:T(8,128)S(1)}, f32[80,256]{1,0:T(8,128)S(1)}, f32[80,256]{1,0:T(8,128)S(1)}, f32[80,256]{1,0:T(8,128)S(1)}) custom-call(s32[2]{0:T(128)S(1)} %pad_add_fusion.ids_ref, f32[64,64]{1,0:T(8,128)S(1)} %basis.1.basis_ref, f32[2,64,256]{2,1,0:T(8,128)S(1)} %add.16.own_ref, ...), custom_call_target="tpu_custom_call" | custom-call | tf_op jit(solution)/shard_map/products/pallas_call | solution.py:264
  22.9 2.1 %collective-permute-start.4 = (f32[80,256]{1,0:T(8,128)S(1)}, f32[80,256]{1,0:T(8,128)S(1)}, u32[]{:S(2)}, u32[]{:S(2)}) collective-permute-start(f32[80,256]{1,0:T(8,128)S(1)} %get-tuple-element.32), channel_id=1, source_target_pairs={{0,4},{4,0},{8,12},{12,8},{1,5},{5,1},{9,13},{13,9},{2,6},{6,2},{1... | collective-permute-start | bytes 245768 | tf_op jit(solution)/shard_map/ppermute | solution.py:495
  25.0 2.6 %collective-permute-start.5 = (f32[80,256]{1,0:T(8,128)S(1)}, f32[80,256]{1,0:T(8,128)S(1)}, u32[]{:S(2)}, u32[]{:S(2)}) collective-permute-start(f32[80,256]{1,0:T(8,128)S(1)} %get-tuple-element.33), channel_id=1, source_target_pairs={{0,8},{4,12},{8,0},{12,4},{1,9},{5,13},{9,1},{13,5},{2,10},{6,14},... | collective-permute-start | bytes 245768 | tf_op jit(solution)/shard_map/ppermute | solution.py:495
  27.6 0.5 collective-permute-done.4.refs_1_
  28.1 6.4 %collective-permute-done.5.refs_2_ = f32[80,256]{1,0:T(8,128)S(1)} collective-permute-done((f32[80,256]{1,0:T(8,128)S(1)}, f32[80,256]{1,0:T(8,128)S(1)}, u32[]{:S(2)}, u32[]{:S(2)}) %collective-permute-start.5) | collective-permute-done | bytes 81952 | tf_op jit(solution)/shard_map/ppermute | solution.py:495
  34.5 2.5 %first_sweep.1 = (f32[64,64]{1,0:T(8,128)S(1)}, f32[4,64,256]{2,1,0:T(8,128)S(1)}, f32[80,256]{1,0:T(8,128)S(1)}) custom-call(f32[80,256]{1,0:T(8,128)S(1)} %get-tuple-element.31.refs_0_, f32[80,256]{1,0:T(8,128)S(1)} %collective-permute-done.4.refs_1_, f32[80,256]{1,0:T(8,128)S(1)} %collective-permute-done.5.refs_2_, ...), custom_call_target="tpu_custom_call" | custom-call | tf_op jit(solution)/shard_map/first_sweep/pallas_call | solution.py:304
  37.1 2.7 %collective-permute-start.9 = (f32[80,256]{1,0:T(8,128)S(1)}, f32[80,256]{1,0:T(8,128)S(1)}, u32[]{:S(2)}, u32[]{:S(2)}) collective-permute-start(f32[80,256]{1,0:T(8,128)S(1)} %get-tuple-element.37.refs_0_), channel_id=1, source_target_pairs={{0,12},{4,8},{8,4},{12,0},{1,13},{5,9},{9,5},{13,1},{2,14},{6,10},... | collective-permute-start | bytes 245768 | tf_op jit(solution)/shard_map/ppermute | solution.py:495
  39.8 0.5 collective-permute-start.8
  40.3 1.2 %collective-permute-start.7 = (f32[80,256]{1,0:T(8,128)S(1)}, f32[80,256]{1,0:T(8,128)S(1)}, u32[]{:S(2)}, u32[]{:S(2)}) collective-permute-start(f32[80,256]{1,0:T(8,128)S(1)} %get-tuple-element.37.refs_0_), channel_id=1, source_target_pairs={{0,4},{4,0},{8,12},{12,8},{1,5},{5,1},{9,13},{13,9},{2,6},{6,2},{1... | collective-permute-start | bytes 245768 | tf_op jit(solution)/shard_map/ppermute | solution.py:495
  41.5 1.5 %collective-permute-start.10 = (f32[64,256]{1,0:T(8,128)S(1)}, f32[64,256]{1,0:T(8,128)S(1)}, u32[]{:S(2)}, u32[]{:S(2)}) collective-permute-start(f32[64,256]{1,0:T(8,128)S(1)} %slice.12.refs_0_), channel_id=1, source_target_pairs={{0,16},{16,0},{1,17},{17,1},{2,18},{18,2},{3,19},{19,3},{4,20},{20... | collective-permute-start | bytes 196616 | tf_op jit(solution)/shard_map/ppermute | solution.py:495
  43.0 1.3 %collective-permute-done.9.refs_3_ = f32[80,256]{1,0:T(8,128)S(1)} collective-permute-done((f32[80,256]{1,0:T(8,128)S(1)}, f32[80,256]{1,0:T(8,128)S(1)}, u32[]{:S(2)}, u32[]{:S(2)}) %collective-permute-start.9) | collective-permute-done | bytes 81952 | tf_op jit(solution)/shard_map/ppermute | solution.py:495
  44.3 1.5 %collective-permute-start.13 = (f32[64,256]{1,0:T(8,128)S(1)}, f32[64,256]{1,0:T(8,128)S(1)}, u32[]{:S(2)}, u32[]{:S(2)}) collective-permute-start(f32[64,256]{1,0:T(8,128)S(1)} %slice.18.refs_3_), channel_id=1, source_target_pairs={{0,16},{16,0},{1,17},{17,1},{2,18},{18,2},{3,19},{19,3},{4,20},{20... | collective-permute-start | bytes 196616 | tf_op jit(solution)/shard_map/ppermute | solution.py:495
  45.8 1.3 %collective-permute-done.8.refs_2_ = f32[80,256]{1,0:T(8,128)S(1)} collective-permute-done((f32[80,256]{1,0:T(8,128)S(1)}, f32[80,256]{1,0:T(8,128)S(1)}, u32[]{:S(2)}, u32[]{:S(2)}) %collective-permute-start.8) | collective-permute-done | bytes 81952 | tf_op jit(solution)/shard_map/ppermute | solution.py:495
  47.1 1.5 %collective-permute-start.12 = (f32[64,256]{1,0:T(8,128)S(1)}, f32[64,256]{1,0:T(8,128)S(1)}, u32[]{:S(2)}, u32[]{:S(2)}) collective-permute-start(f32[64,256]{1,0:T(8,128)S(1)} %slice.17.refs_2_), channel_id=1, source_target_pairs={{0,16},{16,0},{1,17},{17,1},{2,18},{18,2},{3,19},{19,3},{4,20},{20... | collective-permute-start | bytes 196616 | tf_op jit(solution)/shard_map/ppermute | solution.py:495
  48.6 0.6 collective-permute-start.11
  49.2 1.9 %second_sweep.1 = (f32[4,64,256]{2,1,0:T(8,128)S(1)}, f32[64,64]{1,0:T(8,128)S(1)}) custom-call(f32[80,256]{1,0:T(8,128)S(1)} %get-tuple-element.37.refs_0_, f32[80,256]{1,0:T(8,128)S(1)} %collective-permute-done.7.refs_1_, f32[80,256]{1,0:T(8,128)S(1)} %collective-permute-done.8.refs_2_, f32[80,256]{1,0:T(8,128)S(1)} %collective-permute-done.9.refs_3_, ...), custom_call_target="tpu_custom_call" | custom-call | tf_op jit(solution)/shard_map/second_sweep/pallas_call | solution.py:325
  51.1 0.2 collective-permute-done.12.refs_6_
  51.3 1.6 %collective-permute-done.11.refs_5_ = f32[64,256]{1,0:T(8,128)S(1)} collective-permute-done((f32[64,256]{1,0:T(8,128)S(1)}, f32[64,256]{1,0:T(8,128)S(1)}, u32[]{:S(2)}, u32[]{:S(2)}) %collective-permute-start.11) | collective-permute-done | bytes 65568 | tf_op jit(solution)/shard_map/ppermute | solution.py:495
  52.9 0.9 %shared_step.1 = (f32[4,64,256]{2,1,0:T(8,128)S(1)}, f32[64,128]{1,0:T(8,128)S(1)}) custom-call(s32[2]{0:T(128)S(1)} %pad_add_fusion.ids_ref, f32[64,64]{1,0:T(8,128)S(1)} %get-tuple-element.41.both_ref, f32[64,256]{1,0:T(8,128)S(1)} %slice.12.refs_0_, f32[64,256]{1,0:T(8,128)S(1)} %slice.16.refs_1_, f32[64,256]{1,0:T(8,128)S(1)} %slice.17.refs_2_, ...), custom_call_target="tpu_custom_call" | custom-call | tf_op jit(solution)/shard_map/shared_step/pallas_call | solution.py:356
  53.9 1.5 %collective-permute-start.15 = (f32[64,128]{1,0:T(8,128)S(1)}, f32[64,128]{1,0:T(8,128)S(1)}, u32[]{:S(2)}, u32[]{:S(2)}) collective-permute-start(f32[64,128]{1,0:T(8,128)S(1)} %get-tuple-element.43.refs_0_), channel_id=1, source_target_pairs={{0,2},{1,3},{2,0},{3,1},{4,6},{5,7},{6,4},{7,5},{8,10},{9,11},{10,... | collective-permute-start | bytes 98312 | tf_op jit(solution)/shard_map/ppermute | solution.py:495
  55.5 0.3 collective-permute-start.14
  55.8 0.9 %blend.1.refs_4_ = f32[1024,1024]{1,0:T(8,128)S(1)} custom-call(bf16[1,1024,1024]{2,1,0:T(8,128)(2,1)S(1)} %get-tuple-element.26.m_ref, bf16[1,2,1024,1024]{3,2,1,0:T(8,128)(2,1)S(1)} %get-tuple-element.27.g_ref), custom_call_target="tpu_custom_call" | custom-call | tf_op jit(solution)/shard_map/blend/pallas_call | solution.py:387
  56.8 2.6 %momentum_step.1 = bf16[1,1024,1024]{2,1,0:T(8,128)(2,1)} custom-call(s32[2]{0:T(128)S(1)} %pad_add_fusion.ids_ref, f32[4,64,256]{2,1,0:T(8,128)S(1)} %get-tuple-element.40.left_ref, f32[64,64]{1,0:T(8,128)S(1)} %get-tuple-element.41.both_ref, f32[80,256]{1,0:T(8,128)S(1)} %get-tuple-element.37.refs_0_, f32[80,256]{1,0:T(8,128)S(1)} %collective-permute-done.7.refs_1_, ...), custom_call_target="tpu_custom_call" | custom-call | tf_op jit(solution)/shard_map/momentum_step/pallas_call | solution.py:428
  59.4 2.5 %weight_step.1 = (f32[1024,1024]{1,0:T(8,128)}, f32[64,1024]{1,0:T(8,128)}) custom-call(f32[4,64,256]{2,1,0:T(8,128)S(1)} %get-tuple-element.40.left_ref, f32[4,64,256]{2,1,0:T(8,128)S(1)} %get-tuple-element.42.shared_ref, f32[64,128]{1,0:T(8,128)S(1)} %get-tuple-element.43.refs_0_, f32[64,128]{1,0:T(8,128)S(1)} %collective-permute-done.14.refs_1_, ...), custom_call_target="tpu_custom_call" | custom-call | tf_op jit(solution)/shard_map/weight_step/pallas_call | solution.py:474
  (22 shorter events, 0.3 us)
Async XLA Ops:
  4.8 2.3 %collective-permute-start = (f32[2,64,256]{2,1,0:T(8,128)S(1)}, f32[2,64,256]{2,1,0:T(8,128)S(1)}, u32[]{:S(2)}, u32[]{:S(2)}) collective-permute-start(f32[2,64,256]{2,1,0:T(8,128)S(1)} %get-tuple-element.28), channel_id=1, source_target_pairs={{0,1},{1,0},{2,3},{3,2},{4,5},{5,4},{6,7},{7,6},{8,9},{9,8},{10,11... | collective-permute-start | bytes 393224 | tf_op jit(solution)/shard_map/ppermute | solution.py:495
  7.2 5.5 %collective-permute-start.1 = (f32[2,64,256]{2,1,0:T(8,128)S(1)}, f32[2,64,256]{2,1,0:T(8,128)S(1)}, u32[]{:S(2)}, u32[]{:S(2)}) collective-permute-start(f32[2,64,256]{2,1,0:T(8,128)S(1)} %add.14), channel_id=1, source_target_pairs={{0,2},{1,17},{2,0},{3,19},{16,18},{17,1},{18,16},{19,3},{4,6},{5,2... | collective-permute-start | bytes 393224 | tf_op jit(solution)/shard_map/ppermute | solution.py:531
  12.7 5.1 %collective-permute-start.2 = (f32[2,64,256]{2,1,0:T(8,128)S(1)}, f32[2,64,256]{2,1,0:T(8,128)S(1)}, u32[]{:S(2)}, u32[]{:S(2)}) collective-permute-start(f32[2,64,256]{2,1,0:T(8,128)S(1)} %add.15), channel_id=1, source_target_pairs={{0,16},{1,3},{2,18},{3,1},{16,0},{17,19},{18,2},{19,17},{4,20},{5,... | collective-permute-start | bytes 393224 | tf_op jit(solution)/shard_map/ppermute | solution.py:531
  17.8 2.1 %collective-permute-start.3 = (f32[2,64,256]{2,1,0:T(8,128)S(1)}, f32[2,64,256]{2,1,0:T(8,128)S(1)}, u32[]{:S(2)}, u32[]{:S(2)}) collective-permute-start(f32[2,64,256]{2,1,0:T(8,128)S(1)} %add.16.own_ref), channel_id=1, source_target_pairs={{0,1},{1,0},{2,3},{3,2},{4,5},{5,4},{6,7},{7,6},{8,9},{9,8},{10,11... | collective-permute-start | bytes 393224 | tf_op jit(solution)/shard_map/ppermute | solution.py:495
  22.9 5.3 %collective-permute-start.4 = (f32[80,256]{1,0:T(8,128)S(1)}, f32[80,256]{1,0:T(8,128)S(1)}, u32[]{:S(2)}, u32[]{:S(2)}) collective-permute-start(f32[80,256]{1,0:T(8,128)S(1)} %get-tuple-element.32), channel_id=1, source_target_pairs={{0,4},{4,0},{8,12},{12,8},{1,5},{5,1},{9,13},{13,9},{2,6},{6,2},{1... | collective-permute-start | bytes 245768 | tf_op jit(solution)/shard_map/ppermute | solution.py:495
  25.0 9.5 %collective-permute-start.5 = (f32[80,256]{1,0:T(8,128)S(1)}, f32[80,256]{1,0:T(8,128)S(1)}, u32[]{:S(2)}, u32[]{:S(2)}) collective-permute-start(f32[80,256]{1,0:T(8,128)S(1)} %get-tuple-element.33), channel_id=1, source_target_pairs={{0,8},{4,12},{8,0},{12,4},{1,9},{5,13},{9,1},{13,5},{2,10},{6,14},... | collective-permute-start | bytes 245768 | tf_op jit(solution)/shard_map/ppermute | solution.py:495
  27.6 7.0 %collective-permute-start.6 = (f32[80,256]{1,0:T(8,128)S(1)}, f32[80,256]{1,0:T(8,128)S(1)}, u32[]{:S(2)}, u32[]{:S(2)}) collective-permute-start(f32[80,256]{1,0:T(8,128)S(1)} %get-tuple-element.34), channel_id=1, source_target_pairs={{0,12},{4,8},{8,4},{12,0},{1,13},{5,9},{9,5},{13,1},{2,14},{6,10},... | collective-permute-start | bytes 245768 | tf_op jit(solution)/shard_map/ppermute | solution.py:495
  37.1 7.2 %collective-permute-start.9 = (f32[80,256]{1,0:T(8,128)S(1)}, f32[80,256]{1,0:T(8,128)S(1)}, u32[]{:S(2)}, u32[]{:S(2)}) collective-permute-start(f32[80,256]{1,0:T(8,128)S(1)} %get-tuple-element.37.refs_0_), channel_id=1, source_target_pairs={{0,12},{4,8},{8,4},{12,0},{1,13},{5,9},{9,5},{13,1},{2,14},{6,10},... | collective-permute-start | bytes 245768 | tf_op jit(solution)/shard_map/ppermute | solution.py:495
  39.8 7.3 %collective-permute-start.8 = (f32[80,256]{1,0:T(8,128)S(1)}, f32[80,256]{1,0:T(8,128)S(1)}, u32[]{:S(2)}, u32[]{:S(2)}) collective-permute-start(f32[80,256]{1,0:T(8,128)S(1)} %get-tuple-element.37.refs_0_), channel_id=1, source_target_pairs={{0,8},{4,12},{8,0},{12,4},{1,9},{5,13},{9,1},{13,5},{2,10},{6,14},... | collective-permute-start | bytes 245768 | tf_op jit(solution)/shard_map/ppermute | solution.py:495
  40.3 8.3 %collective-permute-start.7 = (f32[80,256]{1,0:T(8,128)S(1)}, f32[80,256]{1,0:T(8,128)S(1)}, u32[]{:S(2)}, u32[]{:S(2)}) collective-permute-start(f32[80,256]{1,0:T(8,128)S(1)} %get-tuple-element.37.refs_0_), channel_id=1, source_target_pairs={{0,4},{4,0},{8,12},{12,8},{1,5},{5,1},{9,13},{13,9},{2,6},{6,2},{1... | collective-permute-start | bytes 245768 | tf_op jit(solution)/shard_map/ppermute | solution.py:495
  41.5 9.6 %collective-permute-start.10 = (f32[64,256]{1,0:T(8,128)S(1)}, f32[64,256]{1,0:T(8,128)S(1)}, u32[]{:S(2)}, u32[]{:S(2)}) collective-permute-start(f32[64,256]{1,0:T(8,128)S(1)} %slice.12.refs_0_), channel_id=1, source_target_pairs={{0,16},{16,0},{1,17},{17,1},{2,18},{18,2},{3,19},{19,3},{4,20},{20... | collective-permute-start | bytes 196616 | tf_op jit(solution)/shard_map/ppermute | solution.py:495
  44.3 6.9 %collective-permute-start.13 = (f32[64,256]{1,0:T(8,128)S(1)}, f32[64,256]{1,0:T(8,128)S(1)}, u32[]{:S(2)}, u32[]{:S(2)}) collective-permute-start(f32[64,256]{1,0:T(8,128)S(1)} %slice.18.refs_3_), channel_id=1, source_target_pairs={{0,16},{16,0},{1,17},{17,1},{2,18},{18,2},{3,19},{19,3},{4,20},{20... | collective-permute-start | bytes 196616 | tf_op jit(solution)/shard_map/ppermute | solution.py:495
  47.1 4.3 %collective-permute-start.12 = (f32[64,256]{1,0:T(8,128)S(1)}, f32[64,256]{1,0:T(8,128)S(1)}, u32[]{:S(2)}, u32[]{:S(2)}) collective-permute-start(f32[64,256]{1,0:T(8,128)S(1)} %slice.17.refs_2_), channel_id=1, source_target_pairs={{0,16},{16,0},{1,17},{17,1},{2,18},{18,2},{3,19},{19,3},{4,20},{20... | collective-permute-start | bytes 196616 | tf_op jit(solution)/shard_map/ppermute | solution.py:495
  48.6 4.3 %collective-permute-start.11 = (f32[64,256]{1,0:T(8,128)S(1)}, f32[64,256]{1,0:T(8,128)S(1)}, u32[]{:S(2)}, u32[]{:S(2)}) collective-permute-start(f32[64,256]{1,0:T(8,128)S(1)} %slice.16.refs_1_), channel_id=1, source_target_pairs={{0,16},{16,0},{1,17},{17,1},{2,18},{18,2},{3,19},{19,3},{4,20},{20... | collective-permute-start | bytes 196616 | tf_op jit(solution)/shard_map/ppermute | solution.py:495
  53.9 5.5 %collective-permute-start.16 = (f32[64,128]{1,0:T(8,128)S(1)}, f32[64,128]{1,0:T(8,128)S(1)}, u32[]{:S(2)}, u32[]{:S(2)}) collective-permute-start(f32[64,128]{1,0:T(8,128)S(1)} %get-tuple-element.43.refs_0_), channel_id=1, source_target_pairs={{0,3},{1,2},{2,1},{3,0},{4,7},{5,6},{6,5},{7,4},{8,11},{9,10},{10,... | collective-permute-start | bytes 98312 | tf_op jit(solution)/shard_map/ppermute | solution.py:495
  53.9 5.4 %collective-permute-start.15 = (f32[64,128]{1,0:T(8,128)S(1)}, f32[64,128]{1,0:T(8,128)S(1)}, u32[]{:S(2)}, u32[]{:S(2)}) collective-permute-start(f32[64,128]{1,0:T(8,128)S(1)} %get-tuple-element.43.refs_0_), channel_id=1, source_target_pairs={{0,2},{1,3},{2,0},{3,1},{4,6},{5,7},{6,4},{7,5},{8,10},{9,11},{10,... | collective-permute-start | bytes 98312 | tf_op jit(solution)/shard_map/ppermute | solution.py:495
  55.5 3.9 %collective-permute-start.14 = (f32[64,128]{1,0:T(8,128)S(1)}, f32[64,128]{1,0:T(8,128)S(1)}, u32[]{:S(2)}, u32[]{:S(2)}) collective-permute-start(f32[64,128]{1,0:T(8,128)S(1)} %get-tuple-element.43.refs_0_), channel_id=1, source_target_pairs={{0,1},{1,0},{2,3},{3,2},{4,5},{5,4},{6,7},{7,6},{8,9},{9,8},{10,11... | collective-permute-start | bytes 98312 | tf_op jit(solution)/shard_map/ppermute | solution.py:495
  56.7 2.6 %copy-start = (f32[1024,1024]{1,0:T(8,128)S(1)}, f32[1024,1024]{1,0:T(8,128)}, u32[]{:S(2)}) copy-start(f32[1024,1024]{1,0:T(8,128)} %refs_4_) | copy-start | bytes 12582916

commit v2 on v1

--- a/solution.py
+++ b/solution.py
@@ -394,50 +394,81 @@
     )(held(momentum), held(grads))
 
 
-def momentum_kernel(size, ids_ref, left_ref, both_ref, *refs):
-    own, refs = refs[:size], refs[size:]
-    blended_ref, out_ref, right_ref, slots_ref, sems = refs
+def factors_kernel(size, ids_ref, left_ref, both_ref, *refs):
+    own, (tall_ref, right_ref) = refs[:size], refs[size:]
     both = decay_part * both_ref[...]
     for s in range(size):
         right_ref[jnp.bitwise_xor(ids_ref[1], s)] = wide(
             exact_dot(both, own[s][: both.shape[0], :])
         )
-    width = right_ref.shape[2]
+    for q in range(left_ref.shape[0]):
+        tall_ref[q] = tall(left_ref[q])
+
+
+def factors(ids, left, both, own):
+    size = len(own)
+    pieces, rank, height = left.shape
+    return pl.pallas_call(
+        functools.partial(factors_kernel, size),
+        out_shape=[
+            jax.ShapeDtypeStruct((pieces, 4 * rank, height), BF16),
+            jax.ShapeDtypeStruct((size, 4 * rank, own[0].shape[1]), BF16),
+        ],
+        in_specs=[SMEM_SPEC] + [VMEM_SPEC] * (2 + size),
+        out_specs=[VMEM_SPEC] * 2,
+        compiler_params=GRANT,
+        name="factors",
+    )(ids, left, both, *own)
+
+
+def momentum_kernel(left_ref, right_ref, blended_ref, out_ref, slots_ref, sems):
+    size, _, width = right_ref.shape
     pieces, _, height = left_ref.shape
     copies = []
     for q in range(pieces):
-        left = tall(left_ref[q])
+        left = left_ref[q]
         down = slice(q * height, (q + 1) * height)
         for j in range(size):
             at = slice(j * width, (j + 1) * width)
             projected = dot(left, right_ref[j], TN)
             slots_ref[q, :, at] = (blended_ref[down, at] - projected).astype(BF16)
-        copies.append(
-            pltpu.make_async_copy(slots_ref.at[q], out_ref.at[0, down, :], sems.at[q])
-        )
-        copies[-1].start()
+            send_out(copies, slots_ref, out_ref.at[0], sems, q, j, size)
     for copy in copies:
         copy.wait()
 
 
-def momentum_step(ids, left, both, own, blended):
-    size = len(own)
-    pieces, rank, height = left.shape
-    width = own[0].shape[1]
+def send_out(copies, slots_ref, out_ref, sems, q, j, size):
+    height, cols = slots_ref.shape[1:]
+    half = size // 2
+    if (j + 1) % half:
+        return
+    side = j // half
+    at = pl.ds(side * (cols // 2), cols // 2)
+    copies.append(
+        pltpu.make_async_copy(
+            slots_ref.at[q, :, at],
+            out_ref.at[pl.ds(q * height, height), at],
+            sems.at[2 * q + side],
+        )
+    )
+    copies[-1].start()
+
+
+def momentum_step(left, right, blended):
+    pieces, _, height = left.shape
     rows, cols = blended.shape
     return pl.pallas_call(
-        functools.partial(momentum_kernel, size),
+        momentum_kernel,
         out_shape=jax.ShapeDtypeStruct((1, rows, cols), BF16),
-        in_specs=[SMEM_SPEC] + [VMEM_SPEC] * (3 + size),
+        in_specs=[VMEM_SPEC] * 3,
         out_specs=HBM_SPEC,
         scratch_shapes=[
-            pltpu.VMEM((size, 4 * rank, width), BF16),
             pltpu.VMEM((pieces, height, cols), BF16),
-            pltpu.SemaphoreType.DMA((pieces,)),
+            pltpu.SemaphoreType.DMA((2 * pieces,)),
         ],
         compiler_params=GRANT,
         name="momentum_step",
-    )(ids, left, both, *own, held(blended))
+    )(left, right, held(blended))
 
 
 def weight_kernel(count, scale, left_ref, shared_ref, *refs):
@@ -453,23 +484,22 @@
         new_right_ref[:, j * width : (j + 1) * width] = new_right
         right_ref[j] = wide(scale * new_right)
     pieces, _, height = left_ref.shape
-    copies = [pltpu.make_async_copy(new_right_ref, new_right_out, sems.at[pieces])]
+    copies = [pltpu.make_async_copy(new_right_ref, new_right_out, sems.at[2 * pieces])]
     copies[-1].start()
     for q in range(pieces):
-        left = tall(left_ref[q])
+        left = left_ref[q]
         down = slice(q * height, (q + 1) * height)
         for j in range(size):
             at = slice(j * width, (j + 1) * width)
             slots_ref[q, :, at] = w_ref[down, at] - dot(left, right_ref[j], TN)
-        copies.append(pltpu.make_async_copy(slots_ref.at[q], out_ref.at[down, :], sems.at[q]))
-        copies[-1].start()
+            send_out(copies, slots_ref, out_ref, sems, q, j, size)
     for copy in copies:
         copy.wait()
 
 
 def weight_step(left, shared, sums, weight, scale):
-    pieces, rank, height = left.shape
-    size, _, width = shared.shape
+    pieces, _, height = left.shape
+    size, rank, width = shared.shape
     _, cols = weight.shape
     return pl.pallas_call(
         functools.partial(weight_kernel, len(sums), scale),
@@ -483,7 +513,7 @@
             pltpu.VMEM((rank, cols), F32),
             pltpu.VMEM((size, 4 * rank, width), BF16),
             pltpu.VMEM((pieces, height, cols), F32),
-            pltpu.SemaphoreType.DMA((pieces + 1,)),
+            pltpu.SemaphoreType.DMA((2 * pieces + 1,)),
         ],
         compiler_params=GRANT,
         name="weight_step",
@@ -548,11 +578,12 @@
         theirs.append(swap(piece, *bits_of("dp")[-1]))
 
     left, both = second_sweep(pieces, factor, first)
+    left_parts, right_parts = factors(ids, left, both, pieces)
     shared, sums = shared_step(ids, both, ours, theirs, replicas)
     sums_all = [sums] + [swap(sums, "tensor", s) for s in range(1, lax.axis_size("tensor"))]
-    new_momentum = momentum_step(ids, left, both, pieces, blended)
+    new_momentum = momentum_step(left_parts, right_parts, blended)
     scale = learn_rate * math.sqrt(ROWS / COLS)
-    new_weight, new_right = weight_step(left, shared, sums_all, weight, scale)
+    new_weight, new_right = weight_step(left_parts, shared, sums_all, weight, scale)
     return (new_weight, new_momentum, new_right)
 
 

time: 62 us -> 61.9 us (level)
    pallas_call x1 -> x2, Pallas kernels: 2.58 us -> 2.56 us  [the longest x1 1.64 us: momentum_step(): pl.pallas_call(momentum_kernel, out_shape=jax.ShapeDtypeStruct((1, rows,...]
where the time goes in v2:
time: 61.9 us; the launch traced here: 61.8 us
  Pallas kernels  22.1 us (36%)
  starting transfers between devices  21.4 us (35%)
  waiting for transfers between devices  17.3 us (28%)
  between operations  0.82 us (1%)
    ppermute x15, starting transfers between devices, swap(): return lax.ppermute(x, axis, [(i, i ^ bit) for i in range(size)])  16.8 us
    ppermute x15, waiting for transfers between devices, swap(): return lax.ppermute(x, axis, [(i, i ^ bit) for i in range(size)])  11.4 us
    ppermute x2, waiting for transfers between devices, step(): own_in = lax.ppermute(own, ('dp', 'tensor'), pairs)  5.89 us
    ppermute x2, starting transfers between devices, step(): own_in = lax.ppermute(own, ('dp', 'tensor'), pairs)  4.67 us
    pallas_call x1, Pallas kernels, load(): pl.pallas_call(functools.partial(load_kernel, replicas), out_shape=[pltpu...  4.11 us
    pallas_call x1, Pallas kernels, products(): pl.pallas_call(functools.partial(products_kernel, size), out_shape=[jax.S...  2.93 us
    pallas_call x1, Pallas kernels, first_sweep(): pl.pallas_call(functools.partial(first_kernel, len(got)), out_shape=[jax....  2.52 us
    pallas_call x1, Pallas kernels, weight_step(): pl.pallas_call(functools.partial(weight_kernel, len(sums), scale), out_sh...  2.42 us
  transfers between devices with their start and end apart: 17, of which 8 were waited for; matrix products, arithmetic and copies ran while one was open for 0% of the time, Pallas kernels for 15%

profile of v2, /device:TPU:0, one launch (start us, length us, event | category | flops | bytes accessed | tf_op | source)
XLA Modules:
  0.0 61.8 jit_solution(10246331414034901756)
XLA Ops:
  0.7 4.1 %load.1 = (bf16[1,1024,1024]{2,1,0:T(8,128)(2,1)S(1)}, bf16[1,2,1024,1024]{3,2,1,0:T(8,128)(2,1)S(1)}, f32[64,1024]{1,0:T(8,128)S(1)}, f32[2,64,256]{2,1,0:T(8,128)S(1)}) custom-call(s32[2]{0:T(128)S(1)} %pad_add_fusion.ids_ref, bf16[1,1024,1024]{2,1,0:T(8,128)(2,1)} %m_hbm.1, bf16[1,2,1024,1024]{3,2,1,0:T(8,128)(2,1)} %g_hbm.1, f32[64,1024]{1,0:T(8,128)} %r_hbm.1), custom_call_target="tpu_custom_call" | custom-call | tf_op jit(solution)/shard_map/load/pallas_call | solution.py:163
  4.8 0.6 collective-permute-start
  5.4 1.7 %raw_half.1 = f32[2,64,256]{2,1,0:T(8,128)S(1)} custom-call(s32[2]{0:T(128)S(1)} %pad_add_fusion.ids_ref, bf16[1,1024,1024]{2,1,0:T(8,128)(2,1)S(1)} %get-tuple-element.28.m_ref, bf16[1,2,1024,1024]{3,2,1,0:T(8,128)(2,1)S(1)} %get-tuple-element.29.g_ref, f32[64,1024]{1,0:T(8,128)S(1)} %get-tuple-element.31.r_ref), custom_call_target="tpu_custom_call" | custom-call | tf_op jit(solution)/shard_map/raw_half/pallas_call | solution.py:209
  7.2 2.6 %collective-permute-start.1 = (f32[2,64,256]{2,1,0:T(8,128)S(1)}, f32[2,64,256]{2,1,0:T(8,128)S(1)}, u32[]{:S(2)}, u32[]{:S(2)}) collective-permute-start(f32[2,64,256]{2,1,0:T(8,128)S(1)} %add.14), channel_id=1, source_target_pairs={{0,2},{1,17},{2,0},{3,19},{16,18},{17,1},{18,16},{19,3},{4,6},{5,2... | collective-permute-start | bytes 393224 | tf_op jit(solution)/shard_map/ppermute | solution.py:561
  9.7 2.9 %collective-permute-done.1 = f32[2,64,256]{2,1,0:T(8,128)S(1)} collective-permute-done((f32[2,64,256]{2,1,0:T(8,128)S(1)}, f32[2,64,256]{2,1,0:T(8,128)S(1)}, u32[]{:S(2)}, u32[]{:S(2)}) %collective-permute-start.1) | collective-permute-done | bytes 131104 | tf_op jit(solution)/shard_map/ppermute | solution.py:561
  12.7 2.1 %collective-permute-start.2 = (f32[2,64,256]{2,1,0:T(8,128)S(1)}, f32[2,64,256]{2,1,0:T(8,128)S(1)}, u32[]{:S(2)}, u32[]{:S(2)}) collective-permute-start(f32[2,64,256]{2,1,0:T(8,128)S(1)} %add.15), channel_id=1, source_target_pairs={{0,16},{1,3},{2,18},{3,1},{16,0},{17,19},{18,2},{19,17},{4,20},{5,... | collective-permute-start | bytes 393224 | tf_op jit(solution)/shard_map/ppermute | solution.py:561
  14.8 2.9 %collective-permute-done.2 = f32[2,64,256]{2,1,0:T(8,128)S(1)} collective-permute-done((f32[2,64,256]{2,1,0:T(8,128)S(1)}, f32[2,64,256]{2,1,0:T(8,128)S(1)}, u32[]{:S(2)}, u32[]{:S(2)}) %collective-permute-start.2) | collective-permute-done | bytes 131104 | tf_op jit(solution)/shard_map/ppermute | solution.py:561
  17.8 2.0 %basis.1.basis_ref = f32[64,64]{1,0:T(8,128)S(1)} custom-call(f32[64,1024]{1,0:T(8,128)S(1)} %get-tuple-element.31.r_ref), custom_call_target="tpu_custom_call" | custom-call | tf_op jit(solution)/shard_map/basis/pallas_call | solution.py:188
  19.9 2.9 %products.1 = (f32[4,64,256]{2,1,0:T(8,128)S(1)}, f32[80,256]{1,0:T(8,128)S(1)}, f32[80,256]{1,0:T(8,128)S(1)}, f32[80,256]{1,0:T(8,128)S(1)}, f32[80,256]{1,0:T(8,128)S(1)}) custom-call(s32[2]{0:T(128)S(1)} %pad_add_fusion.ids_ref, f32[64,64]{1,0:T(8,128)S(1)} %basis.1.basis_ref, f32[2,64,256]{2,1,0:T(8,128)S(1)} %add.16.own_ref, ...), custom_call_target="tpu_custom_call" | custom-call | tf_op jit(solution)/shard_map/products/pallas_call | solution.py:264
  22.9 2.2 %collective-permute-start.4 = (f32[80,256]{1,0:T(8,128)S(1)}, f32[80,256]{1,0:T(8,128)S(1)}, u32[]{:S(2)}, u32[]{:S(2)}) collective-permute-start(f32[80,256]{1,0:T(8,128)S(1)} %get-tuple-element.34), channel_id=1, source_target_pairs={{0,4},{4,0},{8,12},{12,8},{1,5},{5,1},{9,13},{13,9},{2,6},{6,2},{1... | collective-permute-start | bytes 245768 | tf_op jit(solution)/shard_map/ppermute | solution.py:525
  25.0 2.6 %collective-permute-start.5 = (f32[80,256]{1,0:T(8,128)S(1)}, f32[80,256]{1,0:T(8,128)S(1)}, u32[]{:S(2)}, u32[]{:S(2)}) collective-permute-start(f32[80,256]{1,0:T(8,128)S(1)} %get-tuple-element.35), channel_id=1, source_target_pairs={{0,8},{4,12},{8,0},{12,4},{1,9},{5,13},{9,1},{13,5},{2,10},{6,14},... | collective-permute-start | bytes 245768 | tf_op jit(solution)/shard_map/ppermute | solution.py:525
  27.6 0.5 collective-permute-done.4.refs_1_
  28.1 6.4 %collective-permute-done.5.refs_2_ = f32[80,256]{1,0:T(8,128)S(1)} collective-permute-done((f32[80,256]{1,0:T(8,128)S(1)}, f32[80,256]{1,0:T(8,128)S(1)}, u32[]{:S(2)}, u32[]{:S(2)}) %collective-permute-start.5) | collective-permute-done | bytes 81952 | tf_op jit(solution)/shard_map/ppermute | solution.py:525
  34.5 2.5 %first_sweep.1 = (f32[64,64]{1,0:T(8,128)S(1)}, f32[4,64,256]{2,1,0:T(8,128)S(1)}, f32[80,256]{1,0:T(8,128)S(1)}) custom-call(f32[80,256]{1,0:T(8,128)S(1)} %get-tuple-element.33.refs_0_, f32[80,256]{1,0:T(8,128)S(1)} %collective-permute-done.4.refs_1_, f32[80,256]{1,0:T(8,128)S(1)} %collective-permute-done.5.refs_2_, ...), custom_call_target="tpu_custom_call" | custom-call | tf_op jit(solution)/shard_map/first_sweep/pallas_call | solution.py:304
  37.1 2.7 %collective-permute-start.9 = (f32[80,256]{1,0:T(8,128)S(1)}, f32[80,256]{1,0:T(8,128)S(1)}, u32[]{:S(2)}, u32[]{:S(2)}) collective-permute-start(f32[80,256]{1,0:T(8,128)S(1)} %get-tuple-element.39.refs_0_), channel_id=1, source_target_pairs={{0,12},{4,8},{8,4},{12,0},{1,13},{5,9},{9,5},{13,1},{2,14},{6,10},... | collective-permute-start | bytes 245768 | tf_op jit(solution)/shard_map/ppermute | solution.py:525
  39.8 0.5 collective-permute-start.8
  40.3 1.2 %collective-permute-start.7 = (f32[80,256]{1,0:T(8,128)S(1)}, f32[80,256]{1,0:T(8,128)S(1)}, u32[]{:S(2)}, u32[]{:S(2)}) collective-permute-start(f32[80,256]{1,0:T(8,128)S(1)} %get-tuple-element.39.refs_0_), channel_id=1, source_target_pairs={{0,4},{4,0},{8,12},{12,8},{1,5},{5,1},{9,13},{13,9},{2,6},{6,2},{1... | collective-permute-start | bytes 245768 | tf_op jit(solution)/shard_map/ppermute | solution.py:525
  41.5 1.5 %collective-permute-start.10 = (f32[64,256]{1,0:T(8,128)S(1)}, f32[64,256]{1,0:T(8,128)S(1)}, u32[]{:S(2)}, u32[]{:S(2)}) collective-permute-start(f32[64,256]{1,0:T(8,128)S(1)} %slice.12.refs_0_), channel_id=1, source_target_pairs={{0,16},{16,0},{1,17},{17,1},{2,18},{18,2},{3,19},{19,3},{4,20},{20... | collective-permute-start | bytes 196616 | tf_op jit(solution)/shard_map/ppermute | solution.py:525
  43.0 1.3 %collective-permute-done.9.refs_3_ = f32[80,256]{1,0:T(8,128)S(1)} collective-permute-done((f32[80,256]{1,0:T(8,128)S(1)}, f32[80,256]{1,0:T(8,128)S(1)}, u32[]{:S(2)}, u32[]{:S(2)}) %collective-permute-start.9) | collective-permute-done | bytes 81952 | tf_op jit(solution)/shard_map/ppermute | solution.py:525
  44.3 1.5 %collective-permute-start.13 = (f32[64,256]{1,0:T(8,128)S(1)}, f32[64,256]{1,0:T(8,128)S(1)}, u32[]{:S(2)}, u32[]{:S(2)}) collective-permute-start(f32[64,256]{1,0:T(8,128)S(1)} %slice.18.refs_3_), channel_id=1, source_target_pairs={{0,16},{16,0},{1,17},{17,1},{2,18},{18,2},{3,19},{19,3},{4,20},{20... | collective-permute-start | bytes 196616 | tf_op jit(solution)/shard_map/ppermute | solution.py:525
  45.8 1.3 %collective-permute-done.8.refs_2_ = f32[80,256]{1,0:T(8,128)S(1)} collective-permute-done((f32[80,256]{1,0:T(8,128)S(1)}, f32[80,256]{1,0:T(8,128)S(1)}, u32[]{:S(2)}, u32[]{:S(2)}) %collective-permute-start.8) | collective-permute-done | bytes 81952 | tf_op jit(solution)/shard_map/ppermute | solution.py:525
  47.1 1.5 %collective-permute-start.12 = (f32[64,256]{1,0:T(8,128)S(1)}, f32[64,256]{1,0:T(8,128)S(1)}, u32[]{:S(2)}, u32[]{:S(2)}) collective-permute-start(f32[64,256]{1,0:T(8,128)S(1)} %slice.17.refs_2_), channel_id=1, source_target_pairs={{0,16},{16,0},{1,17},{17,1},{2,18},{18,2},{3,19},{19,3},{4,20},{20... | collective-permute-start | bytes 196616 | tf_op jit(solution)/shard_map/ppermute | solution.py:525
  48.6 0.6 collective-permute-start.11
  49.2 1.9 %second_sweep.1 = (f32[4,64,256]{2,1,0:T(8,128)S(1)}, f32[64,64]{1,0:T(8,128)S(1)}) custom-call(f32[80,256]{1,0:T(8,128)S(1)} %get-tuple-element.39.refs_0_, f32[80,256]{1,0:T(8,128)S(1)} %collective-permute-done.7.refs_1_, f32[80,256]{1,0:T(8,128)S(1)} %collective-permute-done.8.refs_2_, f32[80,256]{1,0:T(8,128)S(1)} %collective-permute-done.9.refs_3_, ...), custom_call_target="tpu_custom_call" | custom-call | tf_op jit(solution)/shard_map/second_sweep/pallas_call | solution.py:325
  51.4 1.6 %collective-permute-done.11.refs_5_ = f32[64,256]{1,0:T(8,128)S(1)} collective-permute-done((f32[64,256]{1,0:T(8,128)S(1)}, f32[64,256]{1,0:T(8,128)S(1)}, u32[]{:S(2)}, u32[]{:S(2)}) %collective-permute-start.11) | collective-permute-done | bytes 65568 | tf_op jit(solution)/shard_map/ppermute | solution.py:525
  52.9 0.9 %shared_step.1 = (f32[4,64,256]{2,1,0:T(8,128)S(1)}, f32[64,128]{1,0:T(8,128)S(1)}) custom-call(s32[2]{0:T(128)S(1)} %pad_add_fusion.ids_ref, f32[64,64]{1,0:T(8,128)S(1)} %get-tuple-element.43.both_ref, f32[64,256]{1,0:T(8,128)S(1)} %slice.12.refs_0_, f32[64,256]{1,0:T(8,128)S(1)} %slice.16.refs_1_, f32[64,256]{1,0:T(8,128)S(1)} %slice.17.refs_2_, ...), custom_call_target="tpu_custom_call" | custom-call | tf_op jit(solution)/shard_map/shared_step/pallas_call | solution.py:356
  53.9 1.6 %collective-permute-start.15 = (f32[64,128]{1,0:T(8,128)S(1)}, f32[64,128]{1,0:T(8,128)S(1)}, u32[]{:S(2)}, u32[]{:S(2)}) collective-permute-start(f32[64,128]{1,0:T(8,128)S(1)} %get-tuple-element.46.refs_0_), channel_id=1, source_target_pairs={{0,2},{1,3},{2,0},{3,1},{4,6},{5,7},{6,4},{7,5},{8,10},{9,11},{10,... | collective-permute-start | bytes 98312 | tf_op jit(solution)/shard_map/ppermute | solution.py:525
  55.5 0.3 collective-permute-start.14
  55.8 0.9 %blend.1.blended_ref = f32[1024,1024]{1,0:T(8,128)S(1)} custom-call(bf16[1,1024,1024]{2,1,0:T(8,128)(2,1)S(1)} %get-tuple-element.28.m_ref, bf16[1,2,1024,1024]{3,2,1,0:T(8,128)(2,1)S(1)} %get-tuple-element.29.g_ref), custom_call_target="tpu_custom_call" | custom-call | tf_op jit(solution)/shard_map/blend/pallas_call | solution.py:387
  56.7 0.9 %factors.1 = (bf16[4,256,256]{2,1,0:T(8,128)(2,1)S(1)}, bf16[4,256,256]{2,1,0:T(8,128)(2,1)S(1)}) custom-call(s32[2]{0:T(128)S(1)} %pad_add_fusion.ids_ref, f32[4,64,256]{2,1,0:T(8,128)S(1)} %get-tuple-element.42.left_ref, f32[64,64]{1,0:T(8,128)S(1)} %get-tuple-element.43.both_ref, f32[80,256]{1,0:T(8,128)S(1)} %get-tuple-element.39.refs_0_, ...), custom_call_target="tpu_custom_call" | custom-call | tf_op jit(solution)/shard_map/factors/pallas_call | solution.py:411
  57.7 1.6 %momentum_step.1 = bf16[1,1024,1024]{2,1,0:T(8,128)(2,1)} custom-call(bf16[4,256,256]{2,1,0:T(8,128)(2,1)S(1)} %get-tuple-element.44.left_ref, bf16[4,256,256]{2,1,0:T(8,128)(2,1)S(1)} %get-tuple-element.49.right_ref, f32[1024,1024]{1,0:T(8,128)S(1)} %blend.1.blended_ref), custom_call_target="tpu_custom_call" | custom-call | tf_op jit(solution)/shard_map/momentum_step/pallas_call | solution.py:460
  59.4 2.4 %weight_step.1 = (f32[1024,1024]{1,0:T(8,128)}, f32[64,1024]{1,0:T(8,128)}) custom-call(bf16[4,256,256]{2,1,0:T(8,128)(2,1)S(1)} %get-tuple-element.44.left_ref, f32[4,64,256]{2,1,0:T(8,128)S(1)} %get-tuple-element.45.shared_ref, f32[64,128]{1,0:T(8,128)S(1)} %get-tuple-element.46.refs_0_, f32[64,128]{1,0:T(8,128)S(1)} %collective-permute-done.14.refs_1_, ...), custom_call_target="tpu_custom_call" | custom-call | tf_op jit(solution)/shard_map/weight_step/pallas_call | solution.py:504
  (23 shorter events, 0.5 us)
Async XLA Ops:
  4.8 2.3 %collective-permute-start = (f32[2,64,256]{2,1,0:T(8,128)S(1)}, f32[2,64,256]{2,1,0:T(8,128)S(1)}, u32[]{:S(2)}, u32[]{:S(2)}) collective-permute-start(f32[2,64,256]{2,1,0:T(8,128)S(1)} %get-tuple-element.30), channel_id=1, source_target_pairs={{0,1},{1,0},{2,3},{3,2},{4,5},{5,4},{6,7},{7,6},{8,9},{9,8},{10,11... | collective-permute-start | bytes 393224 | tf_op jit(solution)/shard_map/ppermute | solution.py:525
  7.2 5.5 %collective-permute-start.1 = (f32[2,64,256]{2,1,0:T(8,128)S(1)}, f32[2,64,256]{2,1,0:T(8,128)S(1)}, u32[]{:S(2)}, u32[]{:S(2)}) collective-permute-start(f32[2,64,256]{2,1,0:T(8,128)S(1)} %add.14), channel_id=1, source_target_pairs={{0,2},{1,17},{2,0},{3,19},{16,18},{17,1},{18,16},{19,3},{4,6},{5,2... | collective-permute-start | bytes 393224 | tf_op jit(solution)/shard_map/ppermute | solution.py:561
  12.7 5.1 %collective-permute-start.2 = (f32[2,64,256]{2,1,0:T(8,128)S(1)}, f32[2,64,256]{2,1,0:T(8,128)S(1)}, u32[]{:S(2)}, u32[]{:S(2)}) collective-permute-start(f32[2,64,256]{2,1,0:T(8,128)S(1)} %add.15), channel_id=1, source_target_pairs={{0,16},{1,3},{2,18},{3,1},{16,0},{17,19},{18,2},{19,17},{4,20},{5,... | collective-permute-start | bytes 393224 | tf_op jit(solution)/shard_map/ppermute | solution.py:561
  17.8 2.1 %collective-permute-start.3 = (f32[2,64,256]{2,1,0:T(8,128)S(1)}, f32[2,64,256]{2,1,0:T(8,128)S(1)}, u32[]{:S(2)}, u32[]{:S(2)}) collective-permute-start(f32[2,64,256]{2,1,0:T(8,128)S(1)} %add.16.own_ref), channel_id=1, source_target_pairs={{0,1},{1,0},{2,3},{3,2},{4,5},{5,4},{6,7},{7,6},{8,9},{9,8},{10,11... | collective-permute-start | bytes 393224 | tf_op jit(solution)/shard_map/ppermute | solution.py:525
  22.9 5.3 %collective-permute-start.4 = (f32[80,256]{1,0:T(8,128)S(1)}, f32[80,256]{1,0:T(8,128)S(1)}, u32[]{:S(2)}, u32[]{:S(2)}) collective-permute-start(f32[80,256]{1,0:T(8,128)S(1)} %get-tuple-element.34), channel_id=1, source_target_pairs={{0,4},{4,0},{8,12},{12,8},{1,5},{5,1},{9,13},{13,9},{2,6},{6,2},{1... | collective-permute-start | bytes 245768 | tf_op jit(solution)/shard_map/ppermute | solution.py:525
  25.0 9.5 %collective-permute-start.5 = (f32[80,256]{1,0:T(8,128)S(1)}, f32[80,256]{1,0:T(8,128)S(1)}, u32[]{:S(2)}, u32[]{:S(2)}) collective-permute-start(f32[80,256]{1,0:T(8,128)S(1)} %get-tuple-element.35), channel_id=1, source_target_pairs={{0,8},{4,12},{8,0},{12,4},{1,9},{5,13},{9,1},{13,5},{2,10},{6,14},... | collective-permute-start | bytes 245768 | tf_op jit(solution)/shard_map/ppermute | solution.py:525
  27.6 6.9 %collective-permute-start.6 = (f32[80,256]{1,0:T(8,128)S(1)}, f32[80,256]{1,0:T(8,128)S(1)}, u32[]{:S(2)}, u32[]{:S(2)}) collective-permute-start(f32[80,256]{1,0:T(8,128)S(1)} %get-tuple-element.36), channel_id=1, source_target_pairs={{0,12},{4,8},{8,4},{12,0},{1,13},{5,9},{9,5},{13,1},{2,14},{6,10},... | collective-permute-start | bytes 245768 | tf_op jit(solution)/shard_map/ppermute | solution.py:525
  37.1 7.2 %collective-permute-start.9 = (f32[80,256]{1,0:T(8,128)S(1)}, f32[80,256]{1,0:T(8,128)S(1)}, u32[]{:S(2)}, u32[]{:S(2)}) collective-permute-start(f32[80,256]{1,0:T(8,128)S(1)} %get-tuple-element.39.refs_0_), channel_id=1, source_target_pairs={{0,12},{4,8},{8,4},{12,0},{1,13},{5,9},{9,5},{13,1},{2,14},{6,10},... | collective-permute-start | bytes 245768 | tf_op jit(solution)/shard_map/ppermute | solution.py:525
  39.8 7.3 %collective-permute-start.8 = (f32[80,256]{1,0:T(8,128)S(1)}, f32[80,256]{1,0:T(8,128)S(1)}, u32[]{:S(2)}, u32[]{:S(2)}) collective-permute-start(f32[80,256]{1,0:T(8,128)S(1)} %get-tuple-element.39.refs_0_), channel_id=1, source_target_pairs={{0,8},{4,12},{8,0},{12,4},{1,9},{5,13},{9,1},{13,5},{2,10},{6,14},... | collective-permute-start | bytes 245768 | tf_op jit(solution)/shard_map/ppermute | solution.py:525
  40.3 8.3 %collective-permute-start.7 = (f32[80,256]{1,0:T(8,128)S(1)}, f32[80,256]{1,0:T(8,128)S(1)}, u32[]{:S(2)}, u32[]{:S(2)}) collective-permute-start(f32[80,256]{1,0:T(8,128)S(1)} %get-tuple-element.39.refs_0_), channel_id=1, source_target_pairs={{0,4},{4,0},{8,12},{12,8},{1,5},{5,1},{9,13},{13,9},{2,6},{6,2},{1... | collective-permute-start | bytes 245768 | tf_op jit(solution)/shard_map/ppermute | solution.py:525
  41.5 9.7 %collective-permute-start.10 = (f32[64,256]{1,0:T(8,128)S(1)}, f32[64,256]{1,0:T(8,128)S(1)}, u32[]{:S(2)}, u32[]{:S(2)}) collective-permute-start(f32[64,256]{1,0:T(8,128)S(1)} %slice.12.refs_0_), channel_id=1, source_target_pairs={{0,16},{16,0},{1,17},{17,1},{2,18},{18,2},{3,19},{19,3},{4,20},{20... | collective-permute-start | bytes 196616 | tf_op jit(solution)/shard_map/ppermute | solution.py:525
  44.3 6.9 %collective-permute-start.13 = (f32[64,256]{1,0:T(8,128)S(1)}, f32[64,256]{1,0:T(8,128)S(1)}, u32[]{:S(2)}, u32[]{:S(2)}) collective-permute-start(f32[64,256]{1,0:T(8,128)S(1)} %slice.18.refs_3_), channel_id=1, source_target_pairs={{0,16},{16,0},{1,17},{17,1},{2,18},{18,2},{3,19},{19,3},{4,20},{20... | collective-permute-start | bytes 196616 | tf_op jit(solution)/shard_map/ppermute | solution.py:525
  47.1 4.3 %collective-permute-start.12 = (f32[64,256]{1,0:T(8,128)S(1)}, f32[64,256]{1,0:T(8,128)S(1)}, u32[]{:S(2)}, u32[]{:S(2)}) collective-permute-start(f32[64,256]{1,0:T(8,128)S(1)} %slice.17.refs_2_), channel_id=1, source_target_pairs={{0,16},{16,0},{1,17},{17,1},{2,18},{18,2},{3,19},{19,3},{4,20},{20... | collective-permute-start | bytes 196616 | tf_op jit(solution)/shard_map/ppermute | solution.py:525
  48.6 4.3 %collective-permute-start.11 = (f32[64,256]{1,0:T(8,128)S(1)}, f32[64,256]{1,0:T(8,128)S(1)}, u32[]{:S(2)}, u32[]{:S(2)}) collective-permute-start(f32[64,256]{1,0:T(8,128)S(1)} %slice.16.refs_1_), channel_id=1, source_target_pairs={{0,16},{16,0},{1,17},{17,1},{2,18},{18,2},{3,19},{19,3},{4,20},{20... | collective-permute-start | bytes 196616 | tf_op jit(solution)/shard_map/ppermute | solution.py:525
  53.8 5.5 %collective-permute-start.16 = (f32[64,128]{1,0:T(8,128)S(1)}, f32[64,128]{1,0:T(8,128)S(1)}, u32[]{:S(2)}, u32[]{:S(2)}) collective-permute-start(f32[64,128]{1,0:T(8,128)S(1)} %get-tuple-element.46.refs_0_), channel_id=1, source_target_pairs={{0,3},{1,2},{2,1},{3,0},{4,7},{5,6},{6,5},{7,4},{8,11},{9,10},{10,... | collective-permute-start | bytes 98312 | tf_op jit(solution)/shard_map/ppermute | solution.py:525
  53.9 5.4 %collective-permute-start.15 = (f32[64,128]{1,0:T(8,128)S(1)}, f32[64,128]{1,0:T(8,128)S(1)}, u32[]{:S(2)}, u32[]{:S(2)}) collective-permute-start(f32[64,128]{1,0:T(8,128)S(1)} %get-tuple-element.46.refs_0_), channel_id=1, source_target_pairs={{0,2},{1,3},{2,0},{3,1},{4,6},{5,7},{6,4},{7,5},{8,10},{9,11},{10,... | collective-permute-start | bytes 98312 | tf_op jit(solution)/shard_map/ppermute | solution.py:525
  55.5 3.8 %collective-permute-start.14 = (f32[64,128]{1,0:T(8,128)S(1)}, f32[64,128]{1,0:T(8,128)S(1)}, u32[]{:S(2)}, u32[]{:S(2)}) collective-permute-start(f32[64,128]{1,0:T(8,128)S(1)} %get-tuple-element.46.refs_0_), channel_id=1, source_target_pairs={{0,1},{1,0},{2,3},{3,2},{4,5},{5,4},{6,7},{7,6},{8,9},{9,8},{10,11... | collective-permute-start | bytes 98312 | tf_op jit(solution)/shard_map/ppermute | solution.py:525
  56.7 2.6 %copy-start = (f32[1024,1024]{1,0:T(8,128)S(1)}, f32[1024,1024]{1,0:T(8,128)}, u32[]{:S(2)}) copy-start(f32[1024,1024]{1,0:T(8,128)} %refs_4_) | copy-start | bytes 12582916
